TPU v7x, 768 devices: a whole 4x8x12 slice. The times are simulated.
768 devices in a mesh: ctx: 96 (over x, z, core), tp: 8 (over y).
Axes of the slice: x: 4, y: 8, z: 12, core: 2. Of those that a mesh axis runs over, the one named last changes fastest.
Arguments:
- query: bfloat16 [12288, 8192], P('ctx', 'tp'), may hold values from -6 to 6
- keys: bfloat16 [12288, 8192], P('ctx', 'tp'), may hold values from -6 to 6
- values: bfloat16 [12288, 8192], P('ctx', 'tp'), may hold values from -6 to 6
- rates: float32 [16, 8192], P(None, 'tp'), may hold values from 4.0690105e-05 to 0.03
- residues: float32 [16, 8192], P(None, 'tp'), may hold values from -3 to 3
- skip: float32 [8192], P('tp'), may hold values from 0.25 to 1.5
- gain: float32 [8192], P('tp'), may hold values from 0.25 to 1.75
Outputs:
- mixed: bfloat16 [12288, 8192], P('ctx', 'tp')
All inputs are finite; a program needn't handle non-finite values.
Results may differ from a plain program's by a relative error of at most 0.0025.
Values sent between devices are 32-bit elements; how exact they have to be, the bound alone decides.
A program may use at most 32 MiB of HBM per device.

v0:
```python
import jax
import jax.numpy as jnp
from jax import lax
from jax.sharding import PartitionSpec as P

C = 8192


def combine_pair(first, second):
    return (first[0] * second[0], first[1] * second[0] + second[1])


def body(query, keys, values, rates, residues, skip, gain):
    driven = keys.astype(jnp.float32) * values.astype(jnp.float32)
    count = driven.shape[0]

    def one_mode(total, mode):
        rate, residue = mode
        decay = jnp.exp(-rate)
        scale = residue * jnp.sqrt(1.0 - decay * decay)
        factors = jnp.broadcast_to(decay[None, :], driven.shape)
        state = lax.associative_scan(combine_pair, (factors, driven), axis=0)[1]
        return (total + scale[None, :] * state, state[count - 1])

    start = jnp.zeros(driven.shape, jnp.float32)
    local_part, end_states = lax.scan(one_mode, start, (rates, residues))
    own_index = lax.axis_index("ctx")
    piece = lax.all_gather(end_states[None], "ctx", axis=0, tiled=True)
    number = piece.shape[0]
    sources = jnp.arange(number, dtype=jnp.int32)
    before = sources < own_index
    gaps = jnp.maximum(own_index - 1 - sources, 0).astype(jnp.float32) * count
    weights = jnp.exp(-rates[None, :, :] * gaps[:, None, None])
    weights = jnp.where(before[:, None, None], weights, 0.0)
    carried = jnp.sum(weights * piece, axis=0)
    decay_all = jnp.exp(-rates)
    weighted = residues * jnp.sqrt(1.0 - decay_all * decay_all) * carried
    steps_ahead = jnp.arange(1, count + 1, dtype=jnp.float32)
    powers = jnp.exp(-rates[None, :, :] * steps_ahead[:, None, None])
    filtered = local_part + jnp.sum(powers * weighted[None, :, :], axis=1)
    gated = query.astype(jnp.float32) * (filtered + skip[None, :] * driven)
    partial_sq = jnp.sum(gated * gated, axis=1)
    total_sq = lax.psum(partial_sq, "tp")
    power = total_sq / C
    return (gated * lax.rsqrt(power + 1e-06)[:, None] * gain[None, :]).astype(jnp.bfloat16)


def solution(mesh):
    in_specs = (
        P("ctx", "tp"),
        P("ctx", "tp"),
        P("ctx", "tp"),
        P(None, "tp"),
        P(None, "tp"),
        P("tp"),
        P("tp"),
    )
    out_specs = P("ctx", "tp")
    return jax.shard_map(body, mesh=mesh, in_specs=in_specs, out_specs=out_specs, check_vma=False)
```

profile of v0, /device:TPU:6, one launch (start us, length us, event | category | flops | bytes accessed | tf_op | source)
XLA Modules:
  0.0 238.2 jit_solution(9856649653958994725)
XLA Ops:
  6.5 1.1 convert_multiply_fusion
  7.6 74.1 %while.13 = (s32[]{:T(128)}, f32[128,1024]{1,0:T(8,128)S(1)}, f32[16,1024]{1,0:T(8,128)}, f32[16,1024]{1,0:T(8,128)}, f32[16,1024]{1,0:T(8,128)}, /*index=5*/f32...) while((s32[]{:T(128)}, f32[128,1024]{1,0:T(8,128)S(1)}, f32[16,1024]{1,0:T(8,128)}, ...), condition=%wide.region_1.2_spmd.clone, body=%wide.region_0.1_spmd.clone.sunk | while | flops 1432579 | bytes 14504103 | solution.py:26
  10.9 1.4 dynamic_update_slice.6
  15.5 1.4 dynamic_update_slice.6
  20.1 1.4 dynamic_update_slice.6
  24.8 1.4 dynamic_update_slice.6
  29.4 1.4 dynamic_update_slice.6
  34.0 1.4 dynamic_update_slice.6
  38.6 1.4 dynamic_update_slice.6
  43.3 1.4 dynamic_update_slice.6
  47.9 1.4 dynamic_update_slice.6
  52.5 1.4 dynamic_update_slice.6
  57.2 1.4 dynamic_update_slice.6
  61.8 1.4 dynamic_update_slice.6
  66.4 1.4 dynamic_update_slice.6
  71.0 1.4 dynamic_update_slice.6
  75.7 1.4 dynamic_update_slice.6
  80.3 1.4 dynamic_update_slice.6
  81.8 0.9 neg.11
  82.7 124.1 %all-gather.3.cloned.1.call-done = f32[1536,1024]{1,0:T(8,128)} async-done(((f32[16,1024]{1,0:T(8,128)}), f32[1536,1024]{1,0:T(8,128)}) %all-gather.3.cloned.1.call-update) | async-done | bytes 6291472 | tf_op jit(solution)/shard_map/all_gather | solution.py:28
  206.8 3.6 %multiply_reduce_fusion.1 = f32[16,1024]{1,0:T(8,128)S(1)} fusion(f32[96,16,1024]{2,1,0:T(8,128)} %bitcast.7, f32[96]{0:T(128)S(1)} %convert_multiply_fusion.1, f32[16,1024]{1,0:T(8,128)S(1)} %neg.11, pred[96]{0:T(512)(128)(4,1)S(1)} %iota_compare_fusion), kind=kLoop, calls=%fused_computation.39 | loop fusion | flops 6275072 | bytes 6423008 | tf_op jit(solution)/shard_map/reduce_sum | solution.py:35
  210.5 2.7 %multiply_reduce_fusion = f32[128,1024]{1,0:T(8,128)S(1)} fusion(f32[16,1024]{1,0:T(8,128)S(1)} %multiply_multiply_fusion.4, f32[128]{0:T(128)S(1)} %iota_add_fusion, f32[16,1024]{1,0:T(8,128)S(1)} %neg.11), kind=kLoop, calls=%fused_computation.38 | loop fusion | flops 6160384 | bytes 655872 | tf_op jit(solution)/shard_map/reduce_sum | solution.py:40
  213.5 17.0 %psum.7 = f32[128]{0:T(128)S(1)} all-reduce(f32[128]{0:T(128)S(1)} %get-tuple-element.75), channel_id=1, replica_groups=mesh['ctx'=96,'tp'=8] {'tp'}, use_global_device_ids=true, to_apply=%region_5.6 | all-reduce | flops 128 | bytes 1024 | tf_op jit(solution)/shard_map/psum | solution.py:43
  230.5 0.8 multiply_convert_fusion
  (1032 shorter events, 45.9 us)
Async XLA Ops:
  6.5 200.3 %all-gather.3.cloned.1.call-start = ((), (), s32[]{:S(2)}) async-start(), calls=%async_computation | async-start | bytes 6356992 | tf_op jit(solution)/shard_map/all_gather | solution.py:28
  81.7 128.8 %copy-start.2 = (f32[16,1024]{1,0:T(8,128)S(1)}, f32[16,1024]{1,0:T(8,128)}, u32[]{:S(2)}) copy-start(f32[16,1024]{1,0:T(8,128)} %get-tuple-element.174) | copy-start | bytes 196612
  81.7 128.8 %copy-start.4 = (f32[16,1024]{1,0:T(8,128)S(1)}, f32[16,1024]{1,0:T(8,128)}, u32[]{:S(2)}) copy-start(f32[16,1024]{1,0:T(8,128)} %get-tuple-element.175) | copy-start | bytes 196612
  81.7 131.5 %copy-start = (bf16[128,1024]{1,0:T(8,128)(2,1)S(1)}, bf16[128,1024]{1,0:T(8,128)(2,1)}, u32[]{:S(2)}) copy-start(bf16[128,1024]{1,0:T(8,128)(2,1)} %param.11) | copy-start | bytes 786436
  81.7 131.5 %copy-start.1 = (bf16[128,1024]{1,0:T(8,128)(2,1)S(1)}, bf16[128,1024]{1,0:T(8,128)(2,1)}, u32[]{:S(2)}) copy-start(bf16[128,1024]{1,0:T(8,128)(2,1)} %param.10) | copy-start | bytes 786436
  81.7 131.5 %copy-start.3 = (bf16[128,1024]{1,0:T(8,128)(2,1)S(1)}, bf16[128,1024]{1,0:T(8,128)(2,1)}, u32[]{:S(2)}) copy-start(bf16[128,1024]{1,0:T(8,128)(2,1)} %param.9) | copy-start | bytes 786436
  81.7 131.5 %copy-start.6 = (f32[1024]{0:T(1024)S(1)}, f32[1024]{0:T(1024)}, u32[]{:S(2)}) copy-start(f32[1024]{0:T(1024)} %param.14) | copy-start | bytes 12292
  206.8 23.7 %copy-start.5 = (f32[1024]{0:T(1024)S(1)}, f32[1024]{0:T(1024)}, u32[]{:S(2)}) copy-start(f32[1024]{0:T(1024)} %param.15) | copy-start | bytes 12292
Sparse Core Ops, SparseCore 0:
  81.9 124.9 all-gather.2
where the time goes:
time: 241 us; the launch traced here: 238 us
  waiting for transfers between devices  124 us (51%)
  local copies, waits for them, and re-layouts  42.7 us (18%)
  other arithmetic  34.7 us (14%)
  blocking collectives  17 us (7%)
  between operations  13.5 us (6%)
  loops' own time  6.15 us (3%)
    all_gather x1, waiting for transfers between devices, body(): piece = lax.all_gather(end_states[None], 'ctx', axis=0, tiled=True)  124 us
    dynamic_update_slice x16, local copies, waits for them, and re-layouts, body(): local_part, end_states = lax.scan(one_mode, start, (rates, residues))  22.4 us
    psum x1, blocking collectives, body(): total_sq = lax.psum(partial_sq, 'tp')  17 us
    slice x352, local copies, waits for them, and re-layouts, one_mode(): state = lax.associative_scan(combine_pair, (factors, driven), axis=0)[1]  14.7 us
    mul x16, other arithmetic, one_mode(): scale = residue * jnp.sqrt(1.0 - decay * decay)  12.9 us
    another operation x1, loops' own time, body(): local_part, end_states = lax.scan(one_mode, start, (rates, residues))  6.15 us
    pad x192, local copies, waits for them, and re-layouts, one_mode(): state = lax.associative_scan(combine_pair, (factors, driven), axis=0)[1]  5.63 us
    add x16, other arithmetic, one_mode(): return (total + scale[None, :] * state, state[count - 1])  4.91 us
  transfers between devices with their start and end apart: 1, of which 1 were waited for; matrix products, arithmetic and copies ran while one was open for 0% of the time, Pallas kernels for 0%

commit v1 on v0

v1 whole, which is shorter than its diff:
```python
import functools

import jax
import jax.numpy as jnp
from jax import lax
from jax.experimental import pallas as pl
from jax.experimental.pallas import tpu as pltpu
from jax.sharding import PartitionSpec as P

MESH = pl.DeviceIdType.MESH
F32 = jnp.float32

C = 8192
NX, NZ, NY = 4, 12, 8
LANES = 128
M = 16
COUNT = 128
WIDTH = 1024
LB = WIDTH // LANES
GROUP = 4
GROUPS = NZ // GROUP
MEMBERS = 2 * GROUP
PIECES = 4
PM = M // PIECES
BLOCKS = COUNT // 8


def token_row(block, s):
    return pl.ds(block * 64 + s, 8, stride=8)


def kernel(q_hbm, k_hbm, v_hbm, rates_hbm, res_hbm, skip_hbm, gain_hbm, o_ref,
           q_ref, k_ref, v_ref, rates_ref, res_ref, skip_ref, gain_ref,
           driven, relay, dec, scale, ends, fwd_buf, total, ex_buf, row_total, x_buf,
           start_state, back_src, carry, conv, base, squares, part, parts, inv,
           in_sem, fwd_send, fwd_recv, ex_send, ex_recv, x_send, x_recv,
           back_send, back_recv, y_send, y_recv):
    ctx = lax.axis_index("ctx")
    y = lax.axis_index("tp")
    core = lax.rem(ctx, 2)
    chip = lax.div(ctx, 2)
    z = lax.rem(chip, NZ)
    x = lax.div(chip, NZ)
    g = lax.div(z, GROUP)
    r = lax.rem(z, GROUP)
    me = r * 2 + core
    is_owner = jnp.logical_and(r >= 1, r <= 2)
    my_piece = jnp.where(is_owner, (r - 1) * 2 + core, 0)

    def device(dx, dz, dc, dy):
        return ((dx * NZ + dz) * 2 + dc, dy)

    def owner_device(p):
        return device(x, g * GROUP + 1 + p // 2, p % 2, y)

    def member_device(j):
        return device(x, g * GROUP + j // 2, j % 2, y)

    loads = []
    for n, (src, dst) in enumerate((
            (k_hbm, k_ref), (v_hbm, v_ref), (rates_hbm, rates_ref), (res_hbm, res_ref),
            (q_hbm, q_ref), (skip_hbm, skip_ref), (gain_hbm, gain_ref))):
        load = pltpu.make_async_copy(src, dst, in_sem.at[n])
        load.start()
        loads.append(load)

    barrier = pltpu.get_barrier_semaphore()

    def greet(dev):
        pl.semaphore_signal(barrier, inc=1, device_id=dev, device_id_type=MESH)

    for p in range(PIECES):
        @pl.when(jnp.logical_not(jnp.logical_and(is_owner, my_piece == p)))
        def _(p=p):
            greet(owner_device(p))
    for k in range(1, NY):
        greet(device(x, z, core, lax.rem(y + k, NY)))

    @pl.when(is_owner)
    def _():
        for j in (0, 1, 6, 7):
            greet(member_device(j))
        for k in range(1, GROUPS):
            greet(device(x, lax.rem(z + GROUP * k, NZ), core, y))
        for k in range(1, NX):
            greet(device(lax.rem(x + k, NX), z, core, y))

    loads[2].wait()
    loads[3].wait()
    for which, (src, dst) in enumerate(((rates_ref, dec), (res_ref, scale))):
        for b in range(M // 8):
            for j in range(LB):
                relay[which * 128 + (b * 8 + j) * 8:which * 128 + (b * 8 + j) * 8 + 8, :] = (
                    src[b * 8:b * 8 + 8, j * LANES:(j + 1) * LANES])

    def mode_rate(m):
        return relay[token_row(m // 8, m % 8), :]

    for m in range(M):
        d = jnp.exp(-mode_rate(m))
        dec[m] = d
        scale[m] = relay[pl.ds(128 + (m // 8) * 64 + m % 8, 8, stride=8), :] * jnp.sqrt(1.0 - d * d)

    loads[0].wait()
    loads[1].wait()

    def make_driven(b, _):
        rows = pl.ds(pl.multiple_of(b * 16, 16), 16)
        for j in range(LB):
            cols = slice(j * LANES, (j + 1) * LANES)
            d = k_ref[rows, cols].astype(F32) * v_ref[rows, cols].astype(F32)
            driven[pl.ds(pl.multiple_of(b * 128 + j * 8, 8), 8), :] = d[:8]
            driven[pl.ds(pl.multiple_of(b * 128 + 64 + j * 8, 8), 8), :] = d[8:]
        return 0

    lax.fori_loop(0, COUNT // 16, make_driven, 0)

    def fwd_copy(p):
        return pltpu.make_async_remote_copy(
            src_ref=ends.at[pl.ds(p * PM, PM)], dst_ref=fwd_buf.at[me],
            send_sem=fwd_send.at[p], recv_sem=fwd_recv.at[me],
            device_id=owner_device(p), device_id_type=MESH)

    SEGS = 4
    SEG_BLOCKS = BLOCKS // SEGS

    for p in range(PIECES):
        decays = [dec[p * PM + i] for i in range(PM)]

        def steps(b, states, decays=decays):
            states = list(states)
            for s in range(8):
                for seg in range(SEGS):
                    d = driven[token_row(seg * SEG_BLOCKS + b, s), :]
                    for i in range(PM):
                        n = seg * PM + i
                        states[n] = states[n] * decays[i] + d
            return tuple(states)

        zero = jnp.zeros((8, LANES), F32)
        states = lax.fori_loop(0, SEG_BLOCKS, steps, (zero,) * (SEGS * PM))
        for i in range(PM):
            m = p * PM + i
            leap = jnp.exp(-mode_rate(m) * (COUNT // SEGS))
            s = states[i]
            for seg in range(1, SEGS):
                s = s * leap + states[seg * PM + i]
            ends[m] = s
        if p == 0:
            pl.semaphore_wait(barrier, jnp.where(is_owner, 7 + 7 + GROUPS - 1 + NX - 1, PIECES + 7))

        @pl.when(jnp.logical_not(jnp.logical_and(is_owner, my_piece == p)))
        def _(p=p):
            fwd_copy(p).start()

    def conv_steps(b, states):
        states = list(states)
        for s in range(8):
            d = driven[token_row(b, s), :]
            terms = []
            for m in range(M):
                states[m] = states[m] * dec[m] + d
                terms.append(states[m] * scale[m])
            while len(terms) > 1:
                terms = [terms[i] + terms[i + 1] for i in range(0, len(terms), 2)]
            conv[pl.ds(pl.multiple_of(b * 64 + s * 8, 8), 8), :] = terms[0]
        return tuple(states)

    zero = jnp.zeros((8, LANES), F32)
    lax.fori_loop(0, BLOCKS, conv_steps, (zero,) * M)

    loads[4].wait()
    loads[5].wait()
    loads[6].wait()

    def make_base(b, _):
        rows = pl.ds(pl.multiple_of(b * 16, 16), 16)
        for j in range(LB):
            q = q_ref[rows, j * LANES:(j + 1) * LANES].astype(F32)
            gate = skip_ref[j:j + 1, :]
            for h in range(2):
                at = pl.ds(pl.multiple_of(b * 128 + h * 64 + j * 8, 8), 8)
                local = conv[pl.ds(b * 128 + h * 64 + j, 8, stride=8), :]
                base[at, :] = q[h * 8:h * 8 + 8] * (local + gate * driven[at, :])
        return 0

    lax.fori_loop(0, COUNT // 16, make_base, 0)

    def back_copy(j):
        return pltpu.make_async_remote_copy(
            src_ref=back_src.at[j], dst_ref=carry.at[my_piece],
            send_sem=back_send.at[j], recv_sem=back_recv.at[my_piece],
            device_id=member_device(j), device_id_type=MESH)

    def ex_copy(k):
        return pltpu.make_async_remote_copy(
            src_ref=total, dst_ref=ex_buf.at[k - 1],
            send_sem=ex_send.at[k - 1], recv_sem=ex_recv.at[k - 1],
            device_id=device(x, lax.rem(z + GROUP * k, NZ), core, y), device_id_type=MESH)

    def x_copy(k):
        return pltpu.make_async_remote_copy(
            src_ref=row_total, dst_ref=x_buf.at[x],
            send_sem=x_send.at[k - 1], recv_sem=x_recv.at[x],
            device_id=device(lax.rem(x + k, NX), z, core, y), device_id_type=MESH)

    @pl.when(is_owner)
    def _():
        def rate_of(i):
            m = my_piece * PM + i
            return relay[pl.ds(lax.div(m, 8) * 64 + lax.rem(m, 8), 8, stride=8), :]

        mine = [rate_of(i) for i in range(PM)]
        hop = [jnp.exp(-rt * COUNT) for rt in mine]
        for j in range(MEMBERS):
            @pl.when(me != j)
            def _(j=j):
                pltpu.make_async_remote_copy(
                    src_ref=ends.at[pl.ds(0, PM)], dst_ref=fwd_buf.at[j],
                    send_sem=fwd_send.at[0], recv_sem=fwd_recv.at[j],
                    device_id=member_device(j), device_id_type=MESH).wait_recv()

        @pl.loop(0, PM)
        def _(i):
            fwd_buf[me, i] = ends[my_piece * PM + i]

        for i in range(PM):
            s = fwd_buf[0, i]
            for j in range(1, MEMBERS):
                s = s * hop[i] + fwd_buf[j, i]
            total[i] = s
        for k in range(1, GROUPS):
            ex_copy(k).start()
        for k in range(1, GROUPS):
            ex_copy(k).wait_recv()

        span = float(COUNT * MEMBERS)
        gf = g.astype(F32)
        for i in range(PM):
            rate = mine[i]
            row = total[i] * jnp.exp(-rate * (span * (GROUPS - 1 - gf)))
            before = zero
            for k in range(1, GROUPS):
                src = lax.rem(g - k + GROUPS, GROUPS)
                sf = src.astype(F32)
                row = row + ex_buf[k - 1, i] * jnp.exp(-rate * (span * (GROUPS - 1 - sf)))
                gap = jnp.maximum(gf - 1.0 - sf, 0.0)
                before = before + jnp.where(src < g, 1.0, 0.0) * (ex_buf[k - 1, i] * jnp.exp(-rate * (span * gap)))
            row_total[i] = row
            start_state[i] = before
        for k in range(1, NX):
            @pl.when(x + k < NX)
            def _(k=k):
                x_copy(k).start()
        row_span = span * GROUPS
        for src in range(NX - 1):
            @pl.when(src < x)
            def _(src=src):
                pltpu.make_async_remote_copy(
                    src_ref=row_total, dst_ref=x_buf.at[src],
                    send_sem=x_send.at[0], recv_sem=x_recv.at[src],
                    device_id=device(src, z, core, y), device_id_type=MESH).wait_recv()
                tokens = (x - 1 - src).astype(F32) * row_span + gf * span
                for i in range(PM):
                    start_state[i] = start_state[i] + x_buf[src, i] * jnp.exp(-mine[i] * tokens)
        for j in range(MEMBERS):
            for i in range(PM):
                if j == 0:
                    back_src[0, i] = start_state[i]
                else:
                    back_src[j, i] = back_src[j - 1, i] * hop[i] + fwd_buf[j - 1, i]

            @pl.when(me != j)
            def _(j=j):
                back_copy(j).start()

            @pl.when(me == j)
            def _(j=j):
                for i in range(PM):
                    carry[my_piece, i] = back_src[j, i]

    for p in range(PIECES):
        @pl.when(jnp.logical_not(jnp.logical_and(is_owner, my_piece == p)))
        def _(p=p):
            pltpu.make_async_remote_copy(
                src_ref=back_src.at[0], dst_ref=carry.at[p],
                send_sem=back_send.at[0], recv_sem=back_recv.at[p],
                device_id=owner_device(p), device_id_type=MESH).wait_recv()

    def carry_steps(b, states):
        states = list(states)
        for s in range(8):
            for m in range(M):
                states[m] = states[m] * dec[m]
            terms = states
            while len(terms) > 1:
                terms = [terms[i] + terms[i + 1] for i in range(0, len(terms), 2)]
            conv[pl.ds(pl.multiple_of(b * 64 + s * 8, 8), 8), :] = terms[0]
        return tuple(states)

    lax.fori_loop(0, BLOCKS, carry_steps,
                  tuple(carry[m // PM, m % PM] * scale[m] for m in range(M)))

    def gate_block(b, _):
        rows = pl.ds(pl.multiple_of(b * 16, 16), 16)
        sums = [jnp.zeros((8, LANES), F32)] * 2
        for j in range(LB):
            q = q_ref[rows, j * LANES:(j + 1) * LANES].astype(F32)
            for h in range(2):
                at = pl.ds(pl.multiple_of(b * 128 + h * 64 + j * 8, 8), 8)
                far = conv[pl.ds(b * 128 + h * 64 + j, 8, stride=8), :]
                gated = base[at, :] + q[h * 8:h * 8 + 8] * far
                base[at, :] = gated
                sums[h] = sums[h] + gated * gated
        squares[pl.ds(pl.multiple_of(b * 16, 8), 8), :] = sums[0]
        squares[pl.ds(pl.multiple_of(b * 16 + 8, 8), 8), :] = sums[1]
        return 0

    lax.fori_loop(0, COUNT // 16, gate_block, 0)

    weight = jnp.full((8, LANES), 1.0 / (8 * C), F32)
    part[...] = lax.dot_general(
        weight, squares[...], (((1,), (1,)), ((), ())),
        precision=lax.Precision.HIGHEST, preferred_element_type=F32)

    def y_copy(k):
        return pltpu.make_async_remote_copy(
            src_ref=part, dst_ref=parts.at[y],
            send_sem=y_send.at[k - 1], recv_sem=y_recv.at[y],
            device_id=device(x, z, core, lax.rem(y + k, NY)), device_id_type=MESH)

    for k in range(1, NY):
        y_copy(k).start()
    parts[y] = part[...]
    for k in range(1, NY):
        src = lax.rem(y + k, NY)
        pltpu.make_async_remote_copy(
            src_ref=part, dst_ref=parts.at[src],
            send_sem=y_send.at[0], recv_sem=y_recv.at[src],
            device_id=device(x, z, core, src), device_id_type=MESH).wait_recv()
    power = lax.dot_general(
        parts[...].reshape(NY * 8, LANES), jnp.ones((NY * 8, LANES), F32), (((0,), (0,)), ((), ())),
        precision=lax.Precision.HIGHEST, preferred_element_type=F32)
    inv[...] = lax.rsqrt(power + 1e-06)

    def finish(b, _):
        rows = pl.ds(pl.multiple_of(b * 16, 16), 16)
        for j in range(LB):
            level = gain_ref[j:j + 1, :]
            halves = []
            for h in range(2):
                at = pl.ds(pl.multiple_of(b * 128 + h * 64 + j * 8, 8), 8)
                norm = inv[pl.ds(pl.multiple_of(b * 16 + h * 8, 8), 8), :]
                halves.append(base[at, :] * norm * level)
            o_ref[rows, j * LANES:(j + 1) * LANES] = jnp.concatenate(halves, axis=0).astype(jnp.bfloat16)
        return 0

    lax.fori_loop(0, COUNT // 16, finish, 0)

    for p in range(PIECES):
        @pl.when(jnp.logical_not(jnp.logical_and(is_owner, my_piece == p)))
        def _(p=p):
            fwd_copy(p).wait_send()

    @pl.when(is_owner)
    def _():
        for k in range(1, GROUPS):
            ex_copy(k).wait_send()
        for k in range(1, NX):
            @pl.when(x + k < NX)
            def _(k=k):
                x_copy(k).wait_send()
        for j in range(MEMBERS):
            @pl.when(me != j)
            def _(j=j):
                back_copy(j).wait_send()
    for k in range(1, NY):
        y_copy(k).wait_send()


def body(query, keys, values, rates, residues, skip, gain):
    any_space = pl.BlockSpec(memory_space=pl.ANY)
    vmem = pltpu.VMEM
    dma = pltpu.SemaphoreType.DMA
    tile = (8, LANES)
    return pl.pallas_call(
        kernel,
        name="modal_scan",
        out_shape=jax.ShapeDtypeStruct((COUNT, WIDTH), jnp.bfloat16),
        in_specs=[any_space] * 7,
        out_specs=pl.BlockSpec(memory_space=pltpu.VMEM),
        scratch_shapes=[
            vmem((COUNT, WIDTH), jnp.bfloat16),
            vmem((COUNT, WIDTH), jnp.bfloat16),
            vmem((COUNT, WIDTH), jnp.bfloat16),
            vmem((M, WIDTH), F32),
            vmem((M, WIDTH), F32),
            vmem(tile, F32),
            vmem(tile, F32),
            vmem((COUNT * 8, LANES), F32),
            vmem((256, LANES), F32),
            vmem((M,) + tile, F32),
            vmem((M,) + tile, F32),
            vmem((M,) + tile, F32),
            vmem((MEMBERS, PM) + tile, F32),
            vmem((PM,) + tile, F32),
            vmem((GROUPS - 1, PM) + tile, F32),
            vmem((PM,) + tile, F32),
            vmem((NX, PM) + tile, F32),
            vmem((PM,) + tile, F32),
            vmem((MEMBERS, PM) + tile, F32),
            vmem((PIECES, PM) + tile, F32),
            vmem((COUNT * 8, LANES), F32),
            vmem((COUNT * 8, LANES), F32),
            vmem((COUNT, LANES), F32),
            vmem(tile, F32),
            vmem((NY,) + tile, F32),
            vmem((COUNT, LANES), F32),
            dma((7,)),
            dma((PIECES,)), dma((MEMBERS,)),
            dma((GROUPS - 1,)), dma((GROUPS - 1,)),
            dma((NX - 1,)), dma((NX,)),
            dma((MEMBERS,)), dma((PIECES,)),
            dma((NY - 1,)), dma((NY,)),
        ],
        compiler_params=pltpu.CompilerParams(collective_id=0, has_side_effects=True),
    )(query, keys, values, rates, residues, skip.reshape(LB, LANES), gain.reshape(LB, LANES))


def solution(mesh):
    in_specs = (
        P("ctx", "tp"), P("ctx", "tp"), P("ctx", "tp"),
        P(None, "tp"), P(None, "tp"), P("tp"), P("tp"),
    )
    return jax.shard_map(body, mesh=mesh, in_specs=in_specs, out_specs=P("ctx", "tp"), check_vma=False)
```

time: 241 us -> 40.3 us (0.17); the launches traced: 238 us -> 40.1 us
  waiting for transfers between devices: 124 us -> 0 us
  local copies, waits for them, and re-layouts: 42.7 us -> 1.67 us
  Pallas kernels: 0 us -> 38.5 us
  other arithmetic: 34.7 us -> 0 us
  blocking collectives: 17 us -> 0 us
  between operations: 13.5 us -> 0.01 us
  loops' own time: 6.15 us -> 0 us
    all_gather x1 -> x0, waiting for transfers between devices: 124 us -> none  [body(): piece = lax.all_gather(end_states[None], 'ctx', axis=0, tiled=True)]
    pallas_call x0 -> x1, Pallas kernels: none -> 38.5 us  [body(): pl.pallas_call(kernel, name='modal_scan', out_shape=jax.ShapeDtypeStruct(...]
    dynamic_update_slice x16 -> x0, local copies, waits for them, and re-layouts: 22.4 us -> none  [body(): local_part, end_states = lax.scan(one_mode, start, (rates, residues))]
    psum x1 -> x0, blocking collectives: 17 us -> none  [body(): total_sq = lax.psum(partial_sq, 'tp')]
    slice x352 -> x0, local copies, waits for them, and re-layouts: 14.7 us -> none  [one_mode(): state = lax.associative_scan(combine_pair, (factors, driven), axis=0)[1]]
    mul x35 -> x0, other arithmetic: 14.2 us -> none  [the longest x16 12.9 us: one_mode(): scale = residue * jnp.sqrt(1.0 - decay * decay)]
    add x321 -> x0, other arithmetic: 10.2 us -> none  [the longest x16 4.91 us: one_mode(): return (total + scale[None, :] * state, state[count - 1])]
    reduce_sum x3 -> x0, other arithmetic: 6.58 us -> none  [the longest x1 3.62 us: body(): carried = jnp.sum(weights * piece, axis=0)]
  transfers between devices with their start and end apart: 1 -> 0, of which waited for: 1 -> 0; matrix products, arithmetic and copies ran while one was open for 0% -> 0% of each run, Pallas kernels for 0% -> 0%
where the time goes in v1:
time: 40.3 us; the launch traced here: 40.1 us
  Pallas kernels  38.5 us (96%)
  local copies, waits for them, and re-layouts  1.67 us (4%)
    pallas_call x1, Pallas kernels, body(): pl.pallas_call(kernel, name='modal_scan', out_shape=jax.ShapeDtypeStruct(...  38.5 us
    unnamed x1, local copies, waits for them, and re-layouts  1.67 us

profile of v1, /device:TPU:6, one launch (start us, length us, event | category | flops | bytes accessed | tf_op | source)
XLA Modules:
  0.0 40.1 jit_solution(16812535224603989802)
XLA Ops:
  0.0 38.5 %modal_scan.1 = bf16[128,1024]{1,0:T(8,128)(2,1)} custom-call(bf16[128,1024]{1,0:T(8,128)(2,1)} %q_hbm.1, bf16[128,1024]{1,0:T(8,128)(2,1)} %k_hbm.1, bf16[128,1024]{1,0:T(8,128)(2,1)} %v_hbm.1, f32[16,1024]{1,0:T(8,128)} %rates_hbm.1, f32[16,1024]{1,0:T(8,128)} %res_hbm.1, f32[8,128]{1,0:T(8,128)} %bitcast.2, f32[8,128]{1,0:T(8,128)} %bitcast.3), custom_call_target="tpu_custom_call" | custom-call | tf_op jit(solution)/shard_map/modal_scan/pallas_call | solution.py:386
  38.5 1.7 %copy.9 = bf16[128,1024]{1,0:T(8,128)(2,1)} copy(bf16[128,1024]{1,0:T(8,128)(2,1)} %modal_scan.1) | data formatting | bytes 524288

commit v2 on v1

v2 whole, which is shorter than its diff:
```python
import jax
import jax.numpy as jnp
from jax import lax
from jax.experimental import pallas as pl
from jax.experimental.pallas import tpu as pltpu
from jax.sharding import PartitionSpec as P

MESH = pl.DeviceIdType.MESH
F32 = jnp.float32

C = 8192
NX, NZ, NY = 4, 12, 8
LANES = 128
M = 16
COUNT = 128
WIDTH = 1024
LB = WIDTH // LANES
GROUP = 4
GROUPS = NZ // GROUP
MEMBERS = 2 * GROUP
PIECES = 4
PM = M // PIECES
BLOCKS = COUNT // 8
SEGS = 4
OWNER_BASE = (0, 0, 1)
NEAR = 4
SEG_BLOCKS = BLOCKS // SEGS


def token_row(block, s):
    return pl.ds(block * 64 + s, 8, stride=8)


def kernel(q_hbm, k_hbm, v_hbm, rates_hbm, res_hbm, skip_hbm, g_ref, inv_ref,
           q_ref, k_ref, v_ref, rates_ref, res_ref, skip_ref,
           driven, relay, dec, scale, leap, ends, fwd_buf, total, x_buf, rows_before, rows_with,
           ex_buf, far_buf, far_coef, coef,
           start_state, back_src, carry, conv, base, squares, part, parts,
           in_sem, fwd_send, fwd_recv, x_send, x_recv, ex_send, ex_recv, far_send, far_recv,
           back_send, back_recv, y_send, y_recv, x_ready, ex_ready, y_ready):
    ctx = lax.axis_index("ctx")
    y = lax.axis_index("tp")
    core = lax.rem(ctx, 2)
    chip = lax.div(ctx, 2)
    z = lax.rem(chip, NZ)
    x = lax.div(chip, NZ)
    g = lax.div(z, GROUP)
    r = lax.rem(z, GROUP)
    me = r * 2 + core
    first = g == 0
    owner_base = jnp.where(g == 2, OWNER_BASE[2], OWNER_BASE[0])
    is_owner = jnp.logical_and(r >= owner_base, r <= owner_base + 1)
    pair = jnp.where(r <= owner_base, 0, 1)
    y_rank = jnp.where(y < NY // 2, y, NY + NY // 2 - 1 - y)
    my_piece = pair * 2 + core
    has_rows = x >= 1

    def device(dx, dz, dc, dy):
        return ((dx * NZ + dz) * 2 + dc, dy)

    def owner_device(p):
        return device(x, g * GROUP + owner_base + lax.div(p, 2), lax.rem(p, 2), y)

    def peer_owner(group):
        return device(x, group * GROUP + OWNER_BASE[group] + pair, core, y)

    def is_me(p):
        return jnp.logical_and(is_owner, my_piece == p)

    def member_device(j):
        return device(x, g * GROUP + j // 2, j % 2, y)

    loads = []
    for n, (src, dst) in enumerate((
            (k_hbm, k_ref), (v_hbm, v_ref), (rates_hbm, rates_ref), (res_hbm, res_ref),
            (q_hbm, q_ref), (skip_hbm, skip_ref))):
        load = pltpu.make_async_copy(src, dst, in_sem.at[n])
        load.start()
        loads.append(load)

    barrier = pltpu.get_barrier_semaphore()

    def greet(dev):
        pl.semaphore_signal(barrier, inc=1, device_id=dev, device_id_type=MESH)

    def ready(sem, dev):
        pl.semaphore_signal(sem, inc=1, device_id=dev, device_id_type=MESH)

    def earlier_y(act):
        for k in range(1, NY):
            other = lax.rem(y + k, NY)
            rank = jnp.where(other < NY // 2, other, NY + NY // 2 - 1 - other)

            @pl.when(rank < y_rank)
            def _(other=other):
                act(device(x, z, core, other))

    for p in range(PIECES):
        @pl.when(jnp.logical_not(is_me(p)))
        def _(p=p):
            greet(owner_device(jnp.int32(p)))
    for k in range(1, NY):
        other = lax.rem(y + k, NY)
        rank = jnp.where(other < NY // 2, other, NY + NY // 2 - 1 - other)

        @pl.when(rank > y_rank)
        def _(other=other):
            greet(device(x, z, core, other))

    takes_far = jnp.logical_and(jnp.logical_and(first, r < NEAR // 2), has_rows)

    @pl.when(takes_far)
    def _():
        for group in range(1, GROUPS):
            for p in range(PIECES):
                greet(device(x, group * GROUP + OWNER_BASE[group] + p // 2, p % 2, y))

    @pl.when(is_owner)
    def _():
        for j in range(MEMBERS):
            @pl.when(jnp.logical_or(j // 2 < owner_base, j // 2 > owner_base + 1))
            def _(j=j):
                greet(member_device(j))
        for k in range(1, NX):
            @pl.when(x + k < NX)
            def _(k=k):
                greet(device(lax.rem(x + k, NX), z, core, y))

        @pl.when(first)
        def _():
            greet(peer_owner(1))

        @pl.when(g <= 1)
        def _():
            greet(peer_owner(2))

    expected = y_rank + jnp.where(
        is_owner,
        MEMBERS - 1 + x + g + jnp.where(jnp.logical_and(g >= 1, has_rows), NEAR, 0),
        PIECES)

    loads[2].wait()
    loads[3].wait()
    for which, (src, dst) in enumerate(((rates_ref, dec), (res_ref, scale))):
        for b in range(M // 8):
            for j in range(LB):
                relay[which * 128 + (b * 8 + j) * 8:which * 128 + (b * 8 + j) * 8 + 8, :] = (
                    src[b * 8:b * 8 + 8, j * LANES:(j + 1) * LANES])

    def mode_rate(m):
        return relay[token_row(m // 8, m % 8), :]

    for m in range(M):
        d = jnp.exp(-mode_rate(m))
        dec[m] = d
        leap[m] = jnp.exp(-mode_rate(m) * (COUNT // SEGS))
        scale[m] = relay[pl.ds(128 + (m // 8) * 64 + m % 8, 8, stride=8), :] * jnp.sqrt(1.0 - d * d)

    loads[0].wait()
    loads[1].wait()

    def make_driven(b, _):
        rows = pl.ds(pl.multiple_of(b * 16, 16), 16)
        for j in range(LB):
            cols = slice(j * LANES, (j + 1) * LANES)
            d = k_ref[rows, cols].astype(F32) * v_ref[rows, cols].astype(F32)
            driven[pl.ds(pl.multiple_of(b * 128 + j * 8, 8), 8), :] = d[:8]
            driven[pl.ds(pl.multiple_of(b * 128 + 64 + j * 8, 8), 8), :] = d[8:]
        return 0

    lax.fori_loop(0, COUNT // 16, make_driven, 0)

    def fwd_copy(p):
        return pltpu.make_async_remote_copy(
            src_ref=ends.at[pl.ds(p * PM, PM)], dst_ref=fwd_buf.at[me],
            send_sem=fwd_send.at[p], recv_sem=fwd_recv.at[me],
            device_id=owner_device(p), device_id_type=MESH)

    pl.semaphore_wait(barrier, expected)
    earlier_y(lambda dev: ready(y_ready, dev))

    @pl.when(is_owner)
    def _():
        for src in range(NX - 1):
            @pl.when(src < x)
            def _(src=src):
                ready(x_ready, device(src, z, core, y))

        @pl.when(g >= 1)
        def _():
            ready(ex_ready, peer_owner(0))

        @pl.when(g == 2)
        def _():
            ready(ex_ready, peer_owner(1))

    order = ((1 - pair) * 2, (1 - pair) * 2 + 1, pair * 2 + 1 - core, pair * 2 + core)
    for p in order:
        decays = [dec[p * PM + i] for i in range(PM)]

        def steps(b, states, decays=decays):
            states = list(states)
            for s in range(8):
                for seg in range(SEGS):
                    d = driven[token_row(seg * SEG_BLOCKS + b, s), :]
                    for i in range(PM):
                        n = seg * PM + i
                        states[n] = states[n] * decays[i] + d
            return tuple(states)

        zero = jnp.zeros((8, LANES), F32)
        states = lax.fori_loop(0, SEG_BLOCKS, steps, (zero,) * (SEGS * PM))
        for i in range(PM):
            m = p * PM + i
            s = states[i]
            for seg in range(1, SEGS):
                s = s * leap[m] + states[seg * PM + i]
            ends[m] = s
        @pl.when(jnp.logical_not(is_me(p)))
        def _(p=p):
            fwd_copy(p).start()

    def conv_steps(b, states):
        states = list(states)
        for s in range(8):
            d = driven[token_row(b, s), :]
            terms = []
            for m in range(M):
                states[m] = states[m] * dec[m] + d
                terms.append(states[m] * scale[m])
            while len(terms) > 1:
                terms = [terms[i] + terms[i + 1] for i in range(0, len(terms), 2)]
            conv[pl.ds(pl.multiple_of(b * 64 + s * 8, 8), 8), :] = terms[0]
        return tuple(states)

    zero = jnp.zeros((8, LANES), F32)
    lax.fori_loop(0, BLOCKS, conv_steps, (zero,) * M)

    loads[4].wait()
    loads[5].wait()

    def make_base(b, _):
        rows = pl.ds(pl.multiple_of(b * 16, 16), 16)
        for j in range(LB):
            q = q_ref[rows, j * LANES:(j + 1) * LANES].astype(F32)
            gate = skip_ref[j:j + 1, :]
            for h in range(2):
                at = pl.ds(pl.multiple_of(b * 128 + h * 64 + j * 8, 8), 8)
                local = conv[pl.ds(b * 128 + h * 64 + j, 8, stride=8), :]
                base[at, :] = q[h * 8:h * 8 + 8] * (local + gate * driven[at, :])
        return 0

    lax.fori_loop(0, COUNT // 16, make_base, 0)

    def back_copy(j):
        return pltpu.make_async_remote_copy(
            src_ref=back_src.at[j], dst_ref=carry.at[my_piece],
            send_sem=back_send.at[j], recv_sem=back_recv.at[my_piece],
            device_id=member_device(j), device_id_type=MESH)

    def x_copy(k):
        return pltpu.make_async_remote_copy(
            src_ref=total, dst_ref=x_buf.at[x],
            send_sem=x_send.at[k - 1], recv_sem=x_recv.at[x],
            device_id=device(lax.rem(x + k, NX), z, core, y), device_id_type=MESH)

    def ex_copy(src, group, slot):
        return pltpu.make_async_remote_copy(
            src_ref=src, dst_ref=ex_buf.at[slot],
            send_sem=ex_send.at[slot], recv_sem=ex_recv.at[slot],
            device_id=peer_owner(group), device_id_type=MESH)

    def far_copy(j):
        return pltpu.make_async_remote_copy(
            src_ref=rows_before, dst_ref=far_buf.at[g - 1, my_piece],
            send_sem=far_send.at[j], recv_sem=far_recv.at[g - 1, my_piece],
            device_id=device(x, j // 2, j % 2, y), device_id_type=MESH)

    def far_arrival(group, p):
        return pltpu.make_async_remote_copy(
            src_ref=rows_before, dst_ref=far_buf.at[group - 1, p],
            send_sem=far_send.at[0], recv_sem=far_recv.at[group - 1, p],
            device_id=device(x, group * GROUP + OWNER_BASE[group] + lax.div(p, 2), lax.rem(p, 2), y),
            device_id_type=MESH)

    sends_far = jnp.logical_and(is_owner, jnp.logical_and(g >= 1, has_rows))
    span = COUNT * MEMBERS

    @pl.when(takes_far)
    def _():
        for m in range(M):
            rate = mode_rate(m)
            near = jnp.exp(-rate * (me * COUNT).astype(F32))
            far_coef[1, m] = near
            far_coef[0, m] = near * jnp.exp(-rate * span)

    @pl.when(is_owner)
    def _():
        for i in range(PM):
            m = my_piece * PM + i
            rate = relay[pl.ds(lax.div(m, 8) * 64 + lax.rem(m, 8), 8, stride=8), :]
            coef[0, i] = jnp.exp(-rate * COUNT)
            coef[1, i] = jnp.exp(-rate * span)
            coef[2, i] = jnp.exp(-rate * (2 * span))
            coef[3, i] = jnp.exp(-rate * (GROUPS * span))
            rows_before[i] = zero
            fwd_buf[me, i] = ends[m]
        for j in range(MEMBERS):
            @pl.when(me != j)
            def _(j=j):
                pltpu.make_async_remote_copy(
                    src_ref=ends.at[pl.ds(0, PM)], dst_ref=fwd_buf.at[j],
                    send_sem=fwd_send.at[0], recv_sem=fwd_recv.at[j],
                    device_id=member_device(j), device_id_type=MESH).wait_recv()
        for i in range(PM):
            s = fwd_buf[0, i]
            for j in range(1, MEMBERS):
                s = s * coef[0, i] + fwd_buf[j, i]
            total[i] = s
        @pl.when(x < NX - 1)
        def _():
            pl.semaphore_wait(x_ready, NX - 1 - x)

        for k in range(1, NX):
            @pl.when(x + k < NX)
            def _(k=k):
                x_copy(k).start()
        for src in range(NX - 1):
            @pl.when(src < x)
            def _(src=src):
                pltpu.make_async_remote_copy(
                    src_ref=total, dst_ref=x_buf.at[src],
                    send_sem=x_send.at[0], recv_sem=x_recv.at[src],
                    device_id=device(src, z, core, y), device_id_type=MESH).wait_recv()
                for i in range(PM):
                    rows_before[i] = rows_before[i] * coef[3, i] + x_buf[src, i]

        @pl.when(sends_far)
        def _():
            for j in range(NEAR):
                far_copy(j).start()

        for i in range(PM):
            rows_with[i] = rows_before[i] * coef[3, i] + total[i]
            start_state[i] = rows_before[i] * coef[2, i]

        @pl.when(g <= 1)
        def _():
            pl.semaphore_wait(ex_ready, 2 - g)

        @pl.when(first)
        def _():
            ex_copy(rows_with, 1, 0).start()
            ex_copy(rows_with, 2, 1).start()

        @pl.when(g == 1)
        def _():
            ex_copy(rows_with, 2, 0).start()
            ex_copy(rows_with, 0, 0).wait_recv()
            for i in range(PM):
                start_state[i] = start_state[i] + ex_buf[0, i]

            @pl.when(has_rows)
            def _():
                ex_copy(rows_before, 2, 1).wait_recv()
                for i in range(PM):
                    start_state[i] = start_state[i] + ex_buf[1, i] * coef[1, i]

        @pl.when(g == 2)
        def _():
            @pl.when(has_rows)
            def _():
                ex_copy(rows_before, 1, 1).start()

            for slot in range(2):
                ex_copy(rows_with, 1 - slot, slot).wait_recv()
            for i in range(PM):
                start_state[i] = start_state[i] + ex_buf[0, i] + ex_buf[1, i] * coef[1, i]

        def send_back(j):
            @pl.when(me != j)
            def _():
                back_copy(j).start()

            @pl.when(me == j)
            def _():
                for i in range(PM):
                    carry[my_piece, i] = back_src[j, i]

        for j in range(MEMBERS):
            for i in range(PM):
                if j == 0:
                    back_src[0, i] = start_state[i]
                else:
                    back_src[j, i] = back_src[j - 1, i] * coef[0, i] + fwd_buf[j - 1, i]
            if j < NEAR:
                send_back(j)
            else:
                @pl.when(jnp.logical_not(takes_far))
                def _(j=j):
                    send_back(j)

        @pl.when(takes_far)
        def _():
            for group in range(1, GROUPS):
                far_arrival(group, my_piece).wait_recv()
            for i in range(PM):
                far = far_buf[1, my_piece, i] + far_buf[0, my_piece, i] * coef[1, i]
                for _ in range(NEAR):
                    far = far * coef[0, i]
                for j in range(NEAR, MEMBERS):
                    back_src[j, i] = back_src[j, i] + far
                    far = far * coef[0, i]
            for j in range(NEAR, MEMBERS):
                send_back(j)

    for p in range(PIECES):
        @pl.when(jnp.logical_not(is_me(p)))
        def _(p=p):
            pltpu.make_async_remote_copy(
                src_ref=back_src.at[0], dst_ref=carry.at[p],
                send_sem=back_send.at[0], recv_sem=back_recv.at[p],
                device_id=owner_device(jnp.int32(p)), device_id_type=MESH).wait_recv()

    @pl.when(takes_far)
    def _():
        for p in range(PIECES):
            @pl.when(jnp.logical_not(is_me(p)))
            def _(p=p):
                for group in range(1, GROUPS):
                    far_arrival(group, jnp.int32(p)).wait_recv()
        for m in range(M):
            p, i = m // PM, m % PM
            carry[p, i] = carry[p, i] + far_buf[1, p, i] * far_coef[1, m] + far_buf[0, p, i] * far_coef[0, m]

    def carry_steps(b, states):
        states = list(states)
        for s in range(8):
            for m in range(M):
                states[m] = states[m] * dec[m]
            terms = states
            while len(terms) > 1:
                terms = [terms[i] + terms[i + 1] for i in range(0, len(terms), 2)]
            conv[pl.ds(pl.multiple_of(b * 64 + s * 8, 8), 8), :] = terms[0]
        return tuple(states)

    lax.fori_loop(0, BLOCKS, carry_steps,
                  tuple(carry[m // PM, m % PM] * scale[m] for m in range(M)))

    def gate_block(b, _):
        rows = pl.ds(pl.multiple_of(b * 16, 16), 16)
        sums = [jnp.zeros((8, LANES), F32)] * 2
        for j in range(LB):
            q = q_ref[rows, j * LANES:(j + 1) * LANES].astype(F32)
            for h in range(2):
                at = pl.ds(pl.multiple_of(b * 128 + h * 64 + j * 8, 8), 8)
                far = conv[pl.ds(b * 128 + h * 64 + j, 8, stride=8), :]
                gated = base[at, :] + q[h * 8:h * 8 + 8] * far
                g_ref[pl.ds(pl.multiple_of(b * 16 + h * 8, 8), 8), j * LANES:(j + 1) * LANES] = gated
                sums[h] = sums[h] + gated * gated
        squares[pl.ds(pl.multiple_of(b * 16, 8), 8), :] = sums[0]
        squares[pl.ds(pl.multiple_of(b * 16 + 8, 8), 8), :] = sums[1]
        return 0

    lax.fori_loop(0, COUNT // 16, gate_block, 0)

    weight = jnp.full((8, LANES), 1.0 / (8 * C), F32)
    part[...] = lax.dot_general(
        weight, squares[...], (((1,), (1,)), ((), ())),
        precision=lax.Precision.HIGHEST, preferred_element_type=F32)

    def y_copy(k):
        return pltpu.make_async_remote_copy(
            src_ref=part, dst_ref=parts.at[y],
            send_sem=y_send.at[k - 1], recv_sem=y_recv.at[y],
            device_id=device(x, z, core, lax.rem(y + k, NY)), device_id_type=MESH)

    @pl.when(y_rank < NY - 1)
    def _():
        pl.semaphore_wait(y_ready, NY - 1 - y_rank)

    for k in range(1, NY):
        y_copy(k).start()
    parts[y] = part[...]
    for k in range(1, NY):
        src = lax.rem(y + k, NY)
        pltpu.make_async_remote_copy(
            src_ref=part, dst_ref=parts.at[src],
            send_sem=y_send.at[0], recv_sem=y_recv.at[src],
            device_id=device(x, z, core, src), device_id_type=MESH).wait_recv()
    power = lax.dot_general(
        parts[...].reshape(NY * 8, LANES), jnp.ones((NY * 8, LANES), F32), (((0,), (0,)), ((), ())),
        precision=lax.Precision.HIGHEST, preferred_element_type=F32)
    inv_ref[...] = lax.rsqrt(power + 1e-06)

    for p in range(PIECES):
        @pl.when(jnp.logical_not(is_me(p)))
        def _(p=p):
            fwd_copy(jnp.int32(p)).wait_send()

    @pl.when(is_owner)
    def _():
        for k in range(1, NX):
            @pl.when(x + k < NX)
            def _(k=k):
                x_copy(k).wait_send()
        for j in range(MEMBERS):
            @pl.when(me != j)
            def _(j=j):
                back_copy(j).wait_send()

            if j < NEAR:
                @pl.when(sends_far)
                def _(j=j):
                    far_copy(j).wait_send()

        @pl.when(first)
        def _():
            ex_copy(rows_with, 1, 0).wait_send()
            ex_copy(rows_with, 2, 1).wait_send()

        @pl.when(g == 1)
        def _():
            ex_copy(rows_with, 2, 0).wait_send()

        @pl.when(jnp.logical_and(g == 2, has_rows))
        def _():
            ex_copy(rows_before, 1, 1).wait_send()
    for k in range(1, NY):
        y_copy(k).wait_send()


def scale_rows(g_ref, inv_ref, gain_ref, o_ref):
    def rows_of(b, _):
        rows = pl.ds(pl.multiple_of(b * 16, 16), 16)
        norm = inv_ref[rows, :]
        for j in range(LB):
            cols = slice(j * LANES, (j + 1) * LANES)
            o_ref[rows, cols] = (g_ref[rows, cols] * norm * gain_ref[j:j + 1, :]).astype(jnp.bfloat16)
        return 0

    lax.fori_loop(0, COUNT // 16, rows_of, 0)


def body(query, keys, values, rates, residues, skip, gain):
    in_vmem = lambda a: pltpu.with_memory_space_constraint(a, pltpu.VMEM)
    any_space = pl.BlockSpec(memory_space=pl.ANY)
    vmem = pltpu.VMEM
    dma = pltpu.SemaphoreType.DMA
    tile = (8, LANES)
    piece = (PM,) + tile
    gated, inv = pl.pallas_call(
        kernel,
        name="modal_scan",
        out_shape=(vmem((COUNT, WIDTH), F32), vmem((COUNT, LANES), F32)),
        in_specs=[any_space] * 6,
        out_specs=(pl.BlockSpec(memory_space=pltpu.VMEM), pl.BlockSpec(memory_space=pltpu.VMEM)),
        scratch_shapes=[
            vmem((COUNT, WIDTH), jnp.bfloat16),
            vmem((COUNT, WIDTH), jnp.bfloat16),
            vmem((COUNT, WIDTH), jnp.bfloat16),
            vmem((M, WIDTH), F32),
            vmem((M, WIDTH), F32),
            vmem(tile, F32),
            vmem((COUNT * 8, LANES), F32),
            vmem((256, LANES), F32),
            vmem((M,) + tile, F32),
            vmem((M,) + tile, F32),
            vmem((M,) + tile, F32),
            vmem((M,) + tile, F32),
            vmem((MEMBERS,) + piece, F32),
            vmem(piece, F32),
            vmem((NX,) + piece, F32),
            vmem(piece, F32),
            vmem(piece, F32),
            vmem((2,) + piece, F32),
            vmem((2, PIECES) + piece, F32),
            vmem((2, M) + tile, F32),
            vmem((4,) + piece, F32),
            vmem(piece, F32),
            vmem((MEMBERS,) + piece, F32),
            vmem((PIECES,) + piece, F32),
            vmem((COUNT * 8, LANES), F32),
            vmem((COUNT * 8, LANES), F32),
            vmem((COUNT, LANES), F32),
            vmem(tile, F32),
            vmem((NY,) + tile, F32),
            dma((6,)),
            dma((PIECES,)), dma((MEMBERS,)),
            dma((NX - 1,)), dma((NX,)),
            dma((2,)), dma((2,)),
            dma((MEMBERS,)), dma((2, PIECES)),
            dma((MEMBERS,)), dma((PIECES,)),
            dma((NY - 1,)), dma((NY,)),
            pltpu.SemaphoreType.REGULAR, pltpu.SemaphoreType.REGULAR, pltpu.SemaphoreType.REGULAR,
        ],
        compiler_params=pltpu.CompilerParams(collective_id=0, has_side_effects=True),
    )(query, keys, values, rates, residues, skip.reshape(LB, LANES))
    return pl.pallas_call(
        scale_rows,
        name="scale_rows",
        out_shape=jax.ShapeDtypeStruct((COUNT, WIDTH), jnp.bfloat16),
        in_specs=[pl.BlockSpec(memory_space=pltpu.VMEM)] * 3,
        out_specs=pl.BlockSpec(memory_space=pltpu.VMEM),
    )(in_vmem(gated), in_vmem(inv), gain.reshape(LB, LANES))


def solution(mesh):
    in_specs = (
        P("ctx", "tp"), P("ctx", "tp"), P("ctx", "tp"),
        P(None, "tp"), P(None, "tp"), P("tp"), P("tp"),
    )
    return jax.shard_map(body, mesh=mesh, in_specs=in_specs, out_specs=P("ctx", "tp"), check_vma=False)
```

time: 40.3 us -> 36.7 us (0.911)
  the two profiles are of different devices: /device:TPU:6 before, /device:TPU:134 now
where the time goes in v2:
time: 36.7 us; the launch traced here: 36.5 us
  Pallas kernels  36.5 us (99%)
    pallas_call x1, Pallas kernels, body(): pl.pallas_call(kernel, name='modal_scan', out_shape=(vmem((COUNT, WIDTH),...  35 us
    pallas_call x1, Pallas kernels, body(): pl.pallas_call(scale_rows, name='scale_rows', out_shape=jax.ShapeDtypeStr...  1.48 us

profile of v2, /device:TPU:134, one launch (start us, length us, event | category | flops | bytes accessed | tf_op | source)
XLA Modules:
  0.0 36.5 jit_solution(10939512142637639536)
XLA Ops:
  0.0 35.0 %modal_scan.1 = (f32[128,1024]{1,0:T(8,128)S(1)}, f32[128,128]{1,0:T(8,128)S(1)}) custom-call(bf16[128,1024]{1,0:T(8,128)(2,1)} %q_hbm.1, bf16[128,1024]{1,0:T(8,128)(2,1)} %k_hbm.1, bf16[128,1024]{1,0:T(8,128)(2,1)} %v_hbm.1, f32[16,1024]{1,0:T(8,128)} %rates_hbm.1, f32[16,1024]{1,0:T(8,128)} %res_hbm.1, f32[8,128]{1,0:T(8,128)} %bitcast.2), custom_call_target="tpu_custom_call" | custom-call | tf_op jit(solution)/shard_map/modal_scan/pallas_call | solution.py:552
  35.1 1.5 %scale_rows.1 = bf16[128,1024]{1,0:T(8,128)(2,1)} custom-call(f32[128,1024]{1,0:T(8,128)S(1)} %get-tuple-element.7.g_ref, f32[128,128]{1,0:T(8,128)S(1)} %get-tuple-element.8.inv_ref, f32[8,128]{1,0:T(8,128)} %bitcast.3), custom_call_target="tpu_custom_call" | custom-call | tf_op jit(solution)/shard_map/scale_rows/pallas_call | solution.py:599

commit v3 on v2

--- a/solution.py
+++ b/solution.py
@@ -24,6 +24,7 @@
 SEGS = 4
 OWNER_BASE = (0, 0, 1)
 NEAR = 4
+SCALE_STEPS = 1
 SEG_BLOCKS = BLOCKS // SEGS
 
 
@@ -31,11 +32,11 @@
     return pl.ds(block * 64 + s, 8, stride=8)
 
 
-def kernel(q_hbm, k_hbm, v_hbm, rates_hbm, res_hbm, skip_hbm, g_ref, inv_ref,
-           q_ref, k_ref, v_ref, rates_ref, res_ref, skip_ref,
+def kernel(q_hbm, k_hbm, v_hbm, rates_hbm, res_hbm, skip_hbm, gain_hbm, g_ref, inv_ref,
+           q_ref, k_ref, v_ref, rates_ref, res_ref, skip_ref, gain_ref,
            driven, relay, dec, scale, leap, ends, fwd_buf, total, x_buf, rows_before, rows_with,
            ex_buf, far_buf, far_coef, coef,
-           start_state, back_src, carry, conv, base, squares, part, parts,
+           start_state, back_src, carry, query, conv, base, squares, part, parts,
            in_sem, fwd_send, fwd_recv, x_send, x_recv, ex_send, ex_recv, far_send, far_recv,
            back_send, back_recv, y_send, y_recv, x_ready, ex_ready, y_ready):
     ctx = lax.axis_index("ctx")
@@ -50,7 +51,8 @@
     first = g == 0
     owner_base = jnp.where(g == 2, OWNER_BASE[2], OWNER_BASE[0])
     is_owner = jnp.logical_and(r >= owner_base, r <= owner_base + 1)
-    pair = jnp.where(r <= owner_base, 0, 1)
+    offset = jnp.where(r <= owner_base, 0, 1)
+    pair = jnp.where(g == 1, 1 - offset, offset)
     y_rank = jnp.where(y < NY // 2, y, NY + NY // 2 - 1 - y)
     my_piece = pair * 2 + core
     has_rows = x >= 1
@@ -59,10 +61,15 @@
         return ((dx * NZ + dz) * 2 + dc, dy)
 
     def owner_device(p):
-        return device(x, g * GROUP + owner_base + lax.div(p, 2), lax.rem(p, 2), y)
+        half = lax.div(p, 2)
+        return device(x, g * GROUP + owner_base + jnp.where(g == 1, 1 - half, half), lax.rem(p, 2), y)
+
+    def owner_in(group, p):
+        half = lax.div(p, 2)
+        return device(x, group * GROUP + OWNER_BASE[group] + (1 - half if group == 1 else half), lax.rem(p, 2), y)
 
     def peer_owner(group):
-        return device(x, group * GROUP + OWNER_BASE[group] + pair, core, y)
+        return owner_in(group, my_piece)
 
     def is_me(p):
         return jnp.logical_and(is_owner, my_piece == p)
@@ -73,7 +80,7 @@
     loads = []
     for n, (src, dst) in enumerate((
             (k_hbm, k_ref), (v_hbm, v_ref), (rates_hbm, rates_ref), (res_hbm, res_ref),
-            (q_hbm, q_ref), (skip_hbm, skip_ref))):
+            (q_hbm, q_ref), (skip_hbm, skip_ref), (gain_hbm, gain_ref))):
         load = pltpu.make_async_copy(src, dst, in_sem.at[n])
         load.start()
         loads.append(load)
@@ -113,7 +120,7 @@
     def _():
         for group in range(1, GROUPS):
             for p in range(PIECES):
-                greet(device(x, group * GROUP + OWNER_BASE[group] + p // 2, p % 2, y))
+                greet(owner_in(group, jnp.int32(p)))
 
     @pl.when(is_owner)
     def _():
@@ -176,26 +183,27 @@
             send_sem=fwd_send.at[p], recv_sem=fwd_recv.at[me],
             device_id=owner_device(p), device_id_type=MESH)
 
-    pl.semaphore_wait(barrier, expected)
-    earlier_y(lambda dev: ready(y_ready, dev))
-
-    @pl.when(is_owner)
-    def _():
-        for src in range(NX - 1):
-            @pl.when(src < x)
-            def _(src=src):
-                ready(x_ready, device(src, z, core, y))
-
-        @pl.when(g >= 1)
-        def _():
-            ready(ex_ready, peer_owner(0))
-
-        @pl.when(g == 2)
-        def _():
-            ready(ex_ready, peer_owner(1))
+    def meet():
+        pl.semaphore_wait(barrier, expected)
+        earlier_y(lambda dev: ready(y_ready, dev))
+
+        @pl.when(is_owner)
+        def _():
+            for src in range(NX - 1):
+                @pl.when(src < x)
+                def _(src=src):
+                    ready(x_ready, device(src, z, core, y))
+
+            @pl.when(g >= 1)
+            def _():
+                ready(ex_ready, peer_owner(0))
+
+            @pl.when(g == 2)
+            def _():
+                ready(ex_ready, peer_owner(1))
 
     order = ((1 - pair) * 2, (1 - pair) * 2 + 1, pair * 2 + 1 - core, pair * 2 + core)
-    for p in order:
+    for n_piece, p in enumerate(order):
         decays = [dec[p * PM + i] for i in range(PM)]
 
         def steps(b, states, decays=decays):
@@ -216,9 +224,32 @@
             for seg in range(1, SEGS):
                 s = s * leap[m] + states[seg * PM + i]
             ends[m] = s
-        @pl.when(jnp.logical_not(is_me(p)))
-        def _(p=p):
-            fwd_copy(p).start()
+        if n_piece == 1:
+            meet()
+        if n_piece >= 1:
+            for ready_piece in order[0 if n_piece == 1 else n_piece:n_piece + 1]:
+                @pl.when(jnp.logical_not(is_me(ready_piece)))
+                def _(p=ready_piece):
+                    fwd_copy(p).start()
+
+    loads[4].wait()
+    loads[5].wait()
+    loads[6].wait()
+
+    def make_query(b, _):
+        rows = pl.ds(pl.multiple_of(b * 16, 16), 16)
+        for j in range(LB):
+            q = q_ref[rows, j * LANES:(j + 1) * LANES].astype(F32)
+            query[pl.ds(pl.multiple_of(b * 128 + j * 8, 8), 8), :] = q[:8]
+            query[pl.ds(pl.multiple_of(b * 128 + 64 + j * 8, 8), 8), :] = q[8:]
+        return 0
+
+    lax.fori_loop(0, COUNT // 16, make_query, 0)
+
+    def tree_sum(terms):
+        while len(terms) > 1:
+            terms = [terms[i] + terms[i + 1] for i in range(0, len(terms), 2)]
+        return terms[0]
 
     def conv_steps(b, states):
         states = list(states)
@@ -228,29 +259,12 @@
             for m in range(M):
                 states[m] = states[m] * dec[m] + d
                 terms.append(states[m] * scale[m])
-            while len(terms) > 1:
-                terms = [terms[i] + terms[i + 1] for i in range(0, len(terms), 2)]
-            conv[pl.ds(pl.multiple_of(b * 64 + s * 8, 8), 8), :] = terms[0]
+            local = tree_sum(terms) + skip_ref[...] * d
+            base[pl.ds(pl.multiple_of(b * 64 + s * 8, 8), 8), :] = query[token_row(b, s), :] * local
         return tuple(states)
 
     zero = jnp.zeros((8, LANES), F32)
     lax.fori_loop(0, BLOCKS, conv_steps, (zero,) * M)
-
-    loads[4].wait()
-    loads[5].wait()
-
-    def make_base(b, _):
-        rows = pl.ds(pl.multiple_of(b * 16, 16), 16)
-        for j in range(LB):
-            q = q_ref[rows, j * LANES:(j + 1) * LANES].astype(F32)
-            gate = skip_ref[j:j + 1, :]
-            for h in range(2):
-                at = pl.ds(pl.multiple_of(b * 128 + h * 64 + j * 8, 8), 8)
-                local = conv[pl.ds(b * 128 + h * 64 + j, 8, stride=8), :]
-                base[at, :] = q[h * 8:h * 8 + 8] * (local + gate * driven[at, :])
-        return 0
-
-    lax.fori_loop(0, COUNT // 16, make_base, 0)
 
     def back_copy(j):
         return pltpu.make_async_remote_copy(
@@ -280,7 +294,7 @@
         return pltpu.make_async_remote_copy(
             src_ref=rows_before, dst_ref=far_buf.at[group - 1, p],
             send_sem=far_send.at[0], recv_sem=far_recv.at[group - 1, p],
-            device_id=device(x, group * GROUP + OWNER_BASE[group] + lax.div(p, 2), lax.rem(p, 2), y),
+            device_id=owner_in(group, p),
             device_id_type=MESH)
 
     sends_far = jnp.logical_and(is_owner, jnp.logical_and(g >= 1, has_rows))
@@ -335,27 +349,31 @@
                 for i in range(PM):
                     rows_before[i] = rows_before[i] * coef[3, i] + x_buf[src, i]
 
-        @pl.when(sends_far)
-        def _():
-            for j in range(NEAR):
+        for j in range(NEAR):
+            @pl.when(jnp.logical_and(sends_far, my_piece == j))
+            def _(j=j):
                 far_copy(j).start()
 
         for i in range(PM):
             rows_with[i] = rows_before[i] * coef[3, i] + total[i]
             start_state[i] = rows_before[i] * coef[2, i]
 
-        @pl.when(g <= 1)
-        def _():
-            pl.semaphore_wait(ex_ready, 2 - g)
-
-        @pl.when(first)
-        def _():
-            ex_copy(rows_with, 1, 0).start()
-            ex_copy(rows_with, 2, 1).start()
-
         @pl.when(g == 1)
         def _():
+            pl.semaphore_wait(ex_ready, 1)
             ex_copy(rows_with, 2, 0).start()
+
+        for j in range(NEAR):
+            @pl.when(jnp.logical_and(sends_far, my_piece != j))
+            def _(j=j):
+                far_copy(j).start()
+
+        @pl.when(jnp.logical_and(g == 2, has_rows))
+        def _():
+            ex_copy(rows_before, 1, 1).start()
+
+        @pl.when(g == 1)
+        def _():
             ex_copy(rows_with, 0, 0).wait_recv()
             for i in range(PM):
                 start_state[i] = start_state[i] + ex_buf[0, i]
@@ -368,10 +386,6 @@
 
         @pl.when(g == 2)
         def _():
-            @pl.when(has_rows)
-            def _():
-                ex_copy(rows_before, 1, 1).start()
-
             for slot in range(2):
                 ex_copy(rows_with, 1 - slot, slot).wait_recv()
             for i in range(PM):
@@ -400,74 +414,100 @@
                 def _(j=j):
                     send_back(j)
 
-        @pl.when(takes_far)
-        def _():
-            for group in range(1, GROUPS):
-                far_arrival(group, my_piece).wait_recv()
-            for i in range(PM):
-                far = far_buf[1, my_piece, i] + far_buf[0, my_piece, i] * coef[1, i]
-                for _ in range(NEAR):
-                    far = far * coef[0, i]
-                for j in range(NEAR, MEMBERS):
-                    back_src[j, i] = back_src[j, i] + far
-                    far = far * coef[0, i]
+        @pl.when(first)
+        def _():
+            pl.semaphore_wait(ex_ready, 2)
+            ex_copy(rows_with, 1, 0).start()
+            ex_copy(rows_with, 2, 1).start()
+
+    def serve_behind():
+        for group in range(1, GROUPS):
+            far_arrival(group, my_piece).wait_recv()
+        for i in range(PM):
+            far = far_buf[1, my_piece, i] + far_buf[0, my_piece, i] * coef[1, i]
+            for _ in range(NEAR):
+                far = far * coef[0, i]
             for j in range(NEAR, MEMBERS):
-                send_back(j)
-
-    for p in range(PIECES):
+                back_src[j, i] = back_src[j, i] + far
+                far = far * coef[0, i]
+        for j in range(NEAR, MEMBERS):
+            back_copy(j).start()
+
+    def take(p):
         @pl.when(jnp.logical_not(is_me(p)))
-        def _(p=p):
+        def _():
             pltpu.make_async_remote_copy(
                 src_ref=back_src.at[0], dst_ref=carry.at[p],
                 send_sem=back_send.at[0], recv_sem=back_recv.at[p],
                 device_id=owner_device(jnp.int32(p)), device_id_type=MESH).wait_recv()
 
-    @pl.when(takes_far)
-    def _():
-        for p in range(PIECES):
-            @pl.when(jnp.logical_not(is_me(p)))
-            def _(p=p):
-                for group in range(1, GROUPS):
-                    far_arrival(group, jnp.int32(p)).wait_recv()
-        for m in range(M):
-            p, i = m // PM, m % PM
+    def take_far(p):
+        @pl.when(jnp.logical_not(is_me(p)))
+        def _():
+            for group in range(1, GROUPS):
+                far_arrival(group, jnp.int32(p)).wait_recv()
+
+    def add_far(p):
+        for i in range(PM):
+            m = p * PM + i
             carry[p, i] = carry[p, i] + far_buf[1, p, i] * far_coef[1, m] + far_buf[0, p, i] * far_coef[0, m]
 
-    def carry_steps(b, states):
+    near_owner = jnp.logical_and(is_owner, takes_far)
+
+    def collect(pieces):
+        for p in pieces:
+            take(p)
+
+        @pl.when(takes_far)
+        def _():
+            for p in pieces:
+                take_far(p)
+            for p in pieces:
+                add_far(p)
+
+    def first_steps(b, states):
         states = list(states)
         for s in range(8):
-            for m in range(M):
+            for n in range(M // 2):
+                states[n] = states[n] * dec[M // 2 + n]
+            conv[pl.ds(pl.multiple_of(b * 64 + s * 8, 8), 8), :] = tree_sum(states)
+        return tuple(states)
+
+    def last_steps(b, states):
+        states = list(states)
+        for s in range(8):
+            for m in range(M // 2):
                 states[m] = states[m] * dec[m]
-            terms = states
-            while len(terms) > 1:
-                terms = [terms[i] + terms[i + 1] for i in range(0, len(terms), 2)]
-            conv[pl.ds(pl.multiple_of(b * 64 + s * 8, 8), 8), :] = terms[0]
+            at = pl.ds(pl.multiple_of(b * 64 + s * 8, 8), 8)
+            gated = base[at, :] + query[token_row(b, s), :] * (conv[at, :] + tree_sum(states))
+            base[at, :] = gated
+            conv[at, :] = gated * gated
+        rows = [conv[token_row(b, s), :] for s in range(8)]
+        squares[pl.ds(pl.multiple_of(b * 8, 8), 8), :] = tree_sum(rows)
         return tuple(states)
 
-    lax.fori_loop(0, BLOCKS, carry_steps,
-                  tuple(carry[m // PM, m % PM] * scale[m] for m in range(M)))
-
-    def gate_block(b, _):
-        rows = pl.ds(pl.multiple_of(b * 16, 16), 16)
-        sums = [jnp.zeros((8, LANES), F32)] * 2
-        for j in range(LB):
-            q = q_ref[rows, j * LANES:(j + 1) * LANES].astype(F32)
-            for h in range(2):
-                at = pl.ds(pl.multiple_of(b * 128 + h * 64 + j * 8, 8), 8)
-                far = conv[pl.ds(b * 128 + h * 64 + j, 8, stride=8), :]
-                gated = base[at, :] + q[h * 8:h * 8 + 8] * far
-                g_ref[pl.ds(pl.multiple_of(b * 16 + h * 8, 8), 8), j * LANES:(j + 1) * LANES] = gated
-                sums[h] = sums[h] + gated * gated
-        squares[pl.ds(pl.multiple_of(b * 16, 8), 8), :] = sums[0]
-        squares[pl.ds(pl.multiple_of(b * 16 + 8, 8), 8), :] = sums[1]
-        return 0
-
-    lax.fori_loop(0, COUNT // 16, gate_block, 0)
-
-    weight = jnp.full((8, LANES), 1.0 / (8 * C), F32)
-    part[...] = lax.dot_general(
-        weight, squares[...], (((1,), (1,)), ((), ())),
-        precision=lax.Precision.HIGHEST, preferred_element_type=F32)
+    def starts(pieces):
+        return tuple(carry[p, i] * scale[p * PM + i] for p in pieces for i in range(PM))
+
+    @pl.when(near_owner)
+    def _():
+        serve_behind()
+
+    collect((2, 3))
+    lax.fori_loop(0, BLOCKS, first_steps, starts((2, 3)))
+    collect((0, 1))
+    lax.fori_loop(0, BLOCKS, last_steps, starts((0, 1)))
+
+    def exact_dot(a, b, dims):
+        return lax.dot_general(a, b, (dims, ((), ())), preferred_element_type=F32)
+
+    def split(a):
+        high = a.astype(jnp.bfloat16)
+        return high, (a - high.astype(F32)).astype(jnp.bfloat16)
+
+    weight = jnp.full((8, LANES), 1.0 / (8 * C), jnp.bfloat16)
+    high, low = split(squares[...])
+    part[...] = exact_dot(weight, high, ((1,), (1,))) + exact_dot(weight, low, ((1,), (1,)))
 
     def y_copy(k):
         return pltpu.make_async_remote_copy(
@@ -479,18 +519,26 @@
     def _():
         pl.semaphore_wait(y_ready, NY - 1 - y_rank)
 
-    for k in range(1, NY):
+    for k in (4, 3, 5, 2, 6, 1, 7):
         y_copy(k).start()
     parts[y] = part[...]
+
+    def relayout(b, _):
+        rows = pl.ds(pl.multiple_of(b * 8, 8), 8)
+        for j in range(LB):
+            g_ref[rows, j * LANES:(j + 1) * LANES] = base[token_row(b, j), :] * gain_ref[j:j + 1, :]
+        return 0
+
+    lax.fori_loop(0, BLOCKS, relayout, 0)
     for k in range(1, NY):
         src = lax.rem(y + k, NY)
         pltpu.make_async_remote_copy(
             src_ref=part, dst_ref=parts.at[src],
             send_sem=y_send.at[0], recv_sem=y_recv.at[src],
             device_id=device(x, z, core, src), device_id_type=MESH).wait_recv()
-    power = lax.dot_general(
-        parts[...].reshape(NY * 8, LANES), jnp.ones((NY * 8, LANES), F32), (((0,), (0,)), ((), ())),
-        precision=lax.Precision.HIGHEST, preferred_element_type=F32)
+    unit = jnp.ones((NY * 8, LANES), jnp.bfloat16)
+    high, low = split(parts[...].reshape(NY * 8, LANES))
+    power = exact_dot(high, unit, ((0,), (0,))) + exact_dot(low, unit, ((0,), (0,)))
     inv_ref[...] = lax.rsqrt(power + 1e-06)
 
     for p in range(PIECES):
@@ -530,16 +578,19 @@
         y_copy(k).wait_send()
 
 
-def scale_rows(g_ref, inv_ref, gain_ref, o_ref):
+def scale_rows(g_ref, inv_ref, o_ref):
+    height = COUNT // SCALE_STEPS
+    top = pl.program_id(0) * height
+
     def rows_of(b, _):
-        rows = pl.ds(pl.multiple_of(b * 16, 16), 16)
+        rows = pl.ds(pl.multiple_of(top + b * 16, 16), 16)
         norm = inv_ref[rows, :]
         for j in range(LB):
             cols = slice(j * LANES, (j + 1) * LANES)
-            o_ref[rows, cols] = (g_ref[rows, cols] * norm * gain_ref[j:j + 1, :]).astype(jnp.bfloat16)
+            o_ref[pl.ds(pl.multiple_of(b * 16, 16), 16), cols] = (g_ref[rows, cols] * norm).astype(jnp.bfloat16)
         return 0
 
-    lax.fori_loop(0, COUNT // 16, rows_of, 0)
+    lax.fori_loop(0, height // 16, rows_of, 0)
 
 
 def body(query, keys, values, rates, residues, skip, gain):
@@ -553,7 +604,7 @@
         kernel,
         name="modal_scan",
         out_shape=(vmem((COUNT, WIDTH), F32), vmem((COUNT, LANES), F32)),
-        in_specs=[any_space] * 6,
+        in_specs=[any_space] * 7,
         out_specs=(pl.BlockSpec(memory_space=pltpu.VMEM), pl.BlockSpec(memory_space=pltpu.VMEM)),
         scratch_shapes=[
             vmem((COUNT, WIDTH), jnp.bfloat16),
@@ -561,6 +612,7 @@
             vmem((COUNT, WIDTH), jnp.bfloat16),
             vmem((M, WIDTH), F32),
             vmem((M, WIDTH), F32),
+            vmem(tile, F32),
             vmem(tile, F32),
             vmem((COUNT * 8, LANES), F32),
             vmem((256, LANES), F32),
@@ -582,10 +634,11 @@
             vmem((PIECES,) + piece, F32),
             vmem((COUNT * 8, LANES), F32),
             vmem((COUNT * 8, LANES), F32),
+            vmem((COUNT * 8, LANES), F32),
             vmem((COUNT, LANES), F32),
             vmem(tile, F32),
             vmem((NY,) + tile, F32),
-            dma((6,)),
+            dma((7,)),
             dma((PIECES,)), dma((MEMBERS,)),
             dma((NX - 1,)), dma((NX,)),
             dma((2,)), dma((2,)),
@@ -595,14 +648,15 @@
             pltpu.SemaphoreType.REGULAR, pltpu.SemaphoreType.REGULAR, pltpu.SemaphoreType.REGULAR,
         ],
         compiler_params=pltpu.CompilerParams(collective_id=0, has_side_effects=True),
-    )(query, keys, values, rates, residues, skip.reshape(LB, LANES))
+    )(query, keys, values, rates, residues, skip.reshape(LB, LANES), gain.reshape(LB, LANES))
     return pl.pallas_call(
         scale_rows,
         name="scale_rows",
         out_shape=jax.ShapeDtypeStruct((COUNT, WIDTH), jnp.bfloat16),
-        in_specs=[pl.BlockSpec(memory_space=pltpu.VMEM)] * 3,
-        out_specs=pl.BlockSpec(memory_space=pltpu.VMEM),
-    )(in_vmem(gated), in_vmem(inv), gain.reshape(LB, LANES))
+        grid=(SCALE_STEPS,),
+        in_specs=[pl.BlockSpec(memory_space=pltpu.VMEM)] * 2,
+        out_specs=pl.BlockSpec((COUNT // SCALE_STEPS, WIDTH), lambda n: (n, 0)),
+    )(in_vmem(gated), in_vmem(inv))
 
 
 def solution(mesh):

time: 36.7 us -> 35.1 us (0.956)
  the two profiles are of different devices: /device:TPU:134 before, /device:TPU:6 now
where the time goes in v3:
time: 35.1 us; the launch traced here: 35 us
  Pallas kernels  35 us (100%)
    pallas_call x1, Pallas kernels, body(): pl.pallas_call(kernel, name='modal_scan', out_shape=(vmem((COUNT, WIDTH),...  34.2 us
    pallas_call x1, Pallas kernels, body(): pl.pallas_call(scale_rows, name='scale_rows', out_shape=jax.ShapeDtypeStr...  0.78 us

profile of v3, /device:TPU:6, one launch (start us, length us, event | category | flops | bytes accessed | tf_op | source)
XLA Modules:
  0.0 35.0 jit_solution(16846522742628798091)
XLA Ops:
  0.0 34.2 %modal_scan.1 = (f32[128,1024]{1,0:T(8,128)S(1)}, f32[128,128]{1,0:T(8,128)S(1)}) custom-call(bf16[128,1024]{1,0:T(8,128)(2,1)} %q_hbm.1, bf16[128,1024]{1,0:T(8,128)(2,1)} %k_hbm.1, bf16[128,1024]{1,0:T(8,128)(2,1)} %v_hbm.1, f32[16,1024]{1,0:T(8,128)} %rates_hbm.1, f32[16,1024]{1,0:T(8,128)} %res_hbm.1, f32[8,128]{1,0:T(8,128)} %bitcast.2, f32[8,128]{1,0:T(8,128)} %bitcast.3), custom_call_target="tpu_custom_call" | custom-call | tf_op jit(solution)/shard_map/modal_scan/pallas_call | solution.py:603
  34.2 0.8 %scale_rows.1 = bf16[128,1024]{1,0:T(8,128)(2,1)} custom-call(f32[128,1024]{1,0:T(8,128)S(1)} %get-tuple-element.7.g_ref, f32[128,128]{1,0:T(8,128)S(1)} %get-tuple-element.8.inv_ref), custom_call_target="tpu_custom_call" | custom-call | tf_op jit(solution)/shard_map/scale_rows/pallas_call | solution.py:652

commit v4 on v3

--- a/solution.py
+++ b/solution.py
@@ -24,7 +24,7 @@
 SEGS = 4
 OWNER_BASE = (0, 0, 1)
 NEAR = 4
-SCALE_STEPS = 1
+SCALE_STEPS = 4
 SEG_BLOCKS = BLOCKS // SEGS
 
 
@@ -183,10 +183,7 @@
             send_sem=fwd_send.at[p], recv_sem=fwd_recv.at[me],
             device_id=owner_device(p), device_id_type=MESH)
 
-    def meet():
-        pl.semaphore_wait(barrier, expected)
-        earlier_y(lambda dev: ready(y_ready, dev))
-
+    def answer_rows():
         @pl.when(is_owner)
         def _():
             for src in range(NX - 1):
@@ -194,13 +191,16 @@
                 def _(src=src):
                     ready(x_ready, device(src, z, core, y))
 
-            @pl.when(g >= 1)
-            def _():
-                ready(ex_ready, peer_owner(0))
-
-            @pl.when(g == 2)
-            def _():
-                ready(ex_ready, peer_owner(1))
+    def answer():
+        earlier_y(lambda dev: ready(y_ready, dev))
+
+        @pl.when(jnp.logical_and(is_owner, g >= 1))
+        def _():
+            ready(ex_ready, peer_owner(0))
+
+        @pl.when(jnp.logical_and(is_owner, g == 2))
+        def _():
+            ready(ex_ready, peer_owner(1))
 
     order = ((1 - pair) * 2, (1 - pair) * 2 + 1, pair * 2 + 1 - core, pair * 2 + core)
     for n_piece, p in enumerate(order):
@@ -225,12 +225,15 @@
                 s = s * leap[m] + states[seg * PM + i]
             ends[m] = s
         if n_piece == 1:
-            meet()
+            pl.semaphore_wait(barrier, expected)
         if n_piece >= 1:
             for ready_piece in order[0 if n_piece == 1 else n_piece:n_piece + 1]:
                 @pl.when(jnp.logical_not(is_me(ready_piece)))
                 def _(p=ready_piece):
                     fwd_copy(p).start()
+        if n_piece == 1:
+            answer_rows()
+    answer()
 
     loads[4].wait()
     loads[5].wait()
@@ -530,6 +533,40 @@
         return 0
 
     lax.fori_loop(0, BLOCKS, relayout, 0)
+    for p in range(PIECES):
+        @pl.when(jnp.logical_not(is_me(p)))
+        def _(p=p):
+            fwd_copy(jnp.int32(p)).wait_send()
+
+    @pl.when(is_owner)
+    def _():
+        for k in range(1, NX):
+            @pl.when(x + k < NX)
+            def _(k=k):
+                x_copy(k).wait_send()
+        for j in range(MEMBERS):
+            @pl.when(me != j)
+            def _(j=j):
+                back_copy(j).wait_send()
+
+            if j < NEAR:
+                @pl.when(sends_far)
+                def _(j=j):
+                    far_copy(j).wait_send()
+
+        @pl.when(first)
+        def _():
+            ex_copy(rows_with, 1, 0).wait_send()
+            ex_copy(rows_with, 2, 1).wait_send()
+
+        @pl.when(g == 1)
+        def _():
+            ex_copy(rows_with, 2, 0).wait_send()
+
+        @pl.when(jnp.logical_and(g == 2, has_rows))
+        def _():
+            ex_copy(rows_before, 1, 1).wait_send()
+
     for k in range(1, NY):
         src = lax.rem(y + k, NY)
         pltpu.make_async_remote_copy(
@@ -541,56 +578,27 @@
     power = exact_dot(high, unit, ((0,), (0,))) + exact_dot(low, unit, ((0,), (0,)))
     inv_ref[...] = lax.rsqrt(power + 1e-06)
 
-    for p in range(PIECES):
-        @pl.when(jnp.logical_not(is_me(p)))
-        def _(p=p):
-            fwd_copy(jnp.int32(p)).wait_send()
-
-    @pl.when(is_owner)
-    def _():
-        for k in range(1, NX):
-            @pl.when(x + k < NX)
-            def _(k=k):
-                x_copy(k).wait_send()
-        for j in range(MEMBERS):
-            @pl.when(me != j)
-            def _(j=j):
-                back_copy(j).wait_send()
-
-            if j < NEAR:
-                @pl.when(sends_far)
-                def _(j=j):
-                    far_copy(j).wait_send()
-
-        @pl.when(first)
-        def _():
-            ex_copy(rows_with, 1, 0).wait_send()
-            ex_copy(rows_with, 2, 1).wait_send()
-
-        @pl.when(g == 1)
-        def _():
-            ex_copy(rows_with, 2, 0).wait_send()
-
-        @pl.when(jnp.logical_and(g == 2, has_rows))
-        def _():
-            ex_copy(rows_before, 1, 1).wait_send()
     for k in range(1, NY):
         y_copy(k).wait_send()
 
 
-def scale_rows(g_ref, inv_ref, o_ref):
+def scale_rows(g_ref, inv_ref, o_hbm, rows_ref, sems):
     height = COUNT // SCALE_STEPS
-    top = pl.program_id(0) * height
-
-    def rows_of(b, _):
-        rows = pl.ds(pl.multiple_of(top + b * 16, 16), 16)
-        norm = inv_ref[rows, :]
-        for j in range(LB):
-            cols = slice(j * LANES, (j + 1) * LANES)
-            o_ref[pl.ds(pl.multiple_of(b * 16, 16), 16), cols] = (g_ref[rows, cols] * norm).astype(jnp.bfloat16)
-        return 0
-
-    lax.fori_loop(0, height // 16, rows_of, 0)
+
+    def out_copy(n):
+        part = pl.ds(n * height, height)
+        return pltpu.make_async_copy(rows_ref.at[part], o_hbm.at[part], sems.at[n])
+
+    for n in range(SCALE_STEPS):
+        for b in range(height // 16):
+            rows = slice(n * height + b * 16, n * height + b * 16 + 16)
+            norm = inv_ref[rows, :]
+            for j in range(LB):
+                cols = slice(j * LANES, (j + 1) * LANES)
+                rows_ref[rows, cols] = (g_ref[rows, cols] * norm).astype(jnp.bfloat16)
+        out_copy(n).start()
+    for n in range(SCALE_STEPS):
+        out_copy(n).wait()
 
 
 def body(query, keys, values, rates, residues, skip, gain):
@@ -653,9 +661,9 @@
         scale_rows,
         name="scale_rows",
         out_shape=jax.ShapeDtypeStruct((COUNT, WIDTH), jnp.bfloat16),
-        grid=(SCALE_STEPS,),
         in_specs=[pl.BlockSpec(memory_space=pltpu.VMEM)] * 2,
-        out_specs=pl.BlockSpec((COUNT // SCALE_STEPS, WIDTH), lambda n: (n, 0)),
+        out_specs=pl.BlockSpec(memory_space=pl.ANY),
+        scratch_shapes=[vmem((COUNT, WIDTH), jnp.bfloat16), dma((SCALE_STEPS,))],
     )(in_vmem(gated), in_vmem(inv))
 
 

time: 35.1 us -> 35 us (level)
  no operation moved by 1% of the time
where the time goes in v4:
time: 35 us; the launch traced here: 34.8 us
  Pallas kernels  34.8 us (99%)
    pallas_call x1, Pallas kernels, body(): pl.pallas_call(kernel, name='modal_scan', out_shape=(vmem((COUNT, WIDTH),...  34.1 us
    pallas_call x1, Pallas kernels, body(): pl.pallas_call(scale_rows, name='scale_rows', out_shape=jax.ShapeDtypeStr...  0.74 us

profile of v4, /device:TPU:6, one launch (start us, length us, event | category | flops | bytes accessed | tf_op | source)
XLA Modules:
  0.0 34.8 jit_solution(4665292644719627721)
XLA Ops:
  0.0 34.1 %modal_scan.1 = (f32[128,1024]{1,0:T(8,128)S(1)}, f32[128,128]{1,0:T(8,128)S(1)}) custom-call(bf16[128,1024]{1,0:T(8,128)(2,1)} %q_hbm.1, bf16[128,1024]{1,0:T(8,128)(2,1)} %k_hbm.1, bf16[128,1024]{1,0:T(8,128)(2,1)} %v_hbm.1, f32[16,1024]{1,0:T(8,128)} %rates_hbm.1, f32[16,1024]{1,0:T(8,128)} %res_hbm.1, f32[8,128]{1,0:T(8,128)} %bitcast.2, f32[8,128]{1,0:T(8,128)} %bitcast.3), custom_call_target="tpu_custom_call" | custom-call | tf_op jit(solution)/shard_map/modal_scan/pallas_call | solution.py:611
  34.1 0.7 %scale_rows.1 = bf16[128,1024]{1,0:T(8,128)(2,1)} custom-call(f32[128,1024]{1,0:T(8,128)S(1)} %get-tuple-element.7.g_ref, f32[128,128]{1,0:T(8,128)S(1)} %get-tuple-element.8.inv_ref), custom_call_target="tpu_custom_call" | custom-call | tf_op jit(solution)/shard_map/scale_rows/pallas_call | solution.py:660

commit v5 on v4

--- a/solution.py
+++ b/solution.py
@@ -501,16 +501,12 @@
     collect((0, 1))
     lax.fori_loop(0, BLOCKS, last_steps, starts((0, 1)))
 
-    def exact_dot(a, b, dims):
-        return lax.dot_general(a, b, (dims, ((), ())), preferred_element_type=F32)
-
-    def split(a):
-        high = a.astype(jnp.bfloat16)
-        return high, (a - high.astype(F32)).astype(jnp.bfloat16)
-
-    weight = jnp.full((8, LANES), 1.0 / (8 * C), jnp.bfloat16)
-    high, low = split(squares[...])
-    part[...] = exact_dot(weight, high, ((1,), (1,))) + exact_dot(weight, low, ((1,), (1,)))
+    lane = lax.broadcasted_iota(jnp.int32, (8, LANES), 1)
+    packed = zero
+    for b in range(BLOCKS):
+        row_sum = jnp.sum(squares[b * 8:b * 8 + 8, :], axis=1, keepdims=True)
+        packed = jnp.where(lane == b, row_sum, packed)
+    part[...] = packed * (1.0 / C)
 
     def y_copy(k):
         return pltpu.make_async_remote_copy(
@@ -573,9 +569,7 @@
             src_ref=part, dst_ref=parts.at[src],
             send_sem=y_send.at[0], recv_sem=y_recv.at[src],
             device_id=device(x, z, core, src), device_id_type=MESH).wait_recv()
-    unit = jnp.ones((NY * 8, LANES), jnp.bfloat16)
-    high, low = split(parts[...].reshape(NY * 8, LANES))
-    power = exact_dot(high, unit, ((0,), (0,))) + exact_dot(low, unit, ((0,), (0,)))
+    power = tree_sum([parts[n] for n in range(NY)])
     inv_ref[...] = lax.rsqrt(power + 1e-06)
 
     for k in range(1, NY):
@@ -592,7 +586,9 @@
     for n in range(SCALE_STEPS):
         for b in range(height // 16):
             rows = slice(n * height + b * 16, n * height + b * 16 + 16)
-            norm = inv_ref[rows, :]
+            block = rows.start // 8
+            norm = jnp.concatenate(
+                [jnp.broadcast_to(inv_ref[:, k:k + 1], (8, LANES)) for k in (block, block + 1)], axis=0)
             for j in range(LB):
                 cols = slice(j * LANES, (j + 1) * LANES)
                 rows_ref[rows, cols] = (g_ref[rows, cols] * norm).astype(jnp.bfloat16)
@@ -611,7 +607,7 @@
     gated, inv = pl.pallas_call(
         kernel,
         name="modal_scan",
-        out_shape=(vmem((COUNT, WIDTH), F32), vmem((COUNT, LANES), F32)),
+        out_shape=(vmem((COUNT, WIDTH), F32), vmem(tile, F32)),
         in_specs=[any_space] * 7,
         out_specs=(pl.BlockSpec(memory_space=pltpu.VMEM), pl.BlockSpec(memory_space=pltpu.VMEM)),
         scratch_shapes=[

time: 35 us -> 34.7 us (level)
  no operation moved by 1% of the time
where the time goes in v5:
time: 34.7 us; the launch traced here: 34.6 us
  Pallas kernels  34.6 us (100%)
    pallas_call x1, Pallas kernels, body(): pl.pallas_call(kernel, name='modal_scan', out_shape=(vmem((COUNT, WIDTH),...  33.8 us
    pallas_call x1, Pallas kernels, body(): pl.pallas_call(scale_rows, name='scale_rows', out_shape=jax.ShapeDtypeStr...  0.81 us

profile of v5, /device:TPU:6, one launch (start us, length us, event | category | flops | bytes accessed | tf_op | source)
XLA Modules:
  0.0 34.6 jit_solution(10742300927801193800)
XLA Ops:
  0.0 33.8 %modal_scan.1 = (f32[128,1024]{1,0:T(8,128)S(1)}, f32[8,128]{1,0:T(8,128)S(1)}) custom-call(bf16[128,1024]{1,0:T(8,128)(2,1)} %q_hbm.1, bf16[128,1024]{1,0:T(8,128)(2,1)} %k_hbm.1, bf16[128,1024]{1,0:T(8,128)(2,1)} %v_hbm.1, f32[16,1024]{1,0:T(8,128)} %rates_hbm.1, f32[16,1024]{1,0:T(8,128)} %res_hbm.1, f32[8,128]{1,0:T(8,128)} %bitcast.2, f32[8,128]{1,0:T(8,128)} %bitcast.3), custom_call_target="tpu_custom_call" | custom-call | tf_op jit(solution)/shard_map/modal_scan/pallas_call | solution.py:607
  33.8 0.8 %scale_rows.1 = bf16[128,1024]{1,0:T(8,128)(2,1)} custom-call(f32[128,1024]{1,0:T(8,128)S(1)} %get-tuple-element.7.g_ref, f32[8,128]{1,0:T(8,128)S(1)} %get-tuple-element.8.inv_ref), custom_call_target="tpu_custom_call" | custom-call | tf_op jit(solution)/shard_map/scale_rows/pallas_call | solution.py:656

commit v6 on v5

--- a/solution.py
+++ b/solution.py
@@ -38,7 +38,7 @@
            ex_buf, far_buf, far_coef, coef,
            start_state, back_src, carry, query, conv, base, squares, part, parts,
            in_sem, fwd_send, fwd_recv, x_send, x_recv, ex_send, ex_recv, far_send, far_recv,
-           back_send, back_recv, y_send, y_recv, x_ready, ex_ready, y_ready):
+           back_send, back_recv, y_send, y_recv, x_ready, ex_ready, y_ready, back_ready):
     ctx = lax.axis_index("ctx")
     y = lax.axis_index("tp")
     core = lax.rem(ctx, 2)
@@ -102,32 +102,36 @@
             def _(other=other):
                 act(device(x, z, core, other))
 
+    is_late = r > owner_base + 1
     for p in range(PIECES):
-        @pl.when(jnp.logical_not(is_me(p)))
+        @pl.when(jnp.logical_not(jnp.logical_or(is_me(p), is_late)))
         def _(p=p):
             greet(owner_device(jnp.int32(p)))
-    for k in range(1, NY):
-        other = lax.rem(y + k, NY)
-        rank = jnp.where(other < NY // 2, other, NY + NY // 2 - 1 - other)
-
-        @pl.when(rank > y_rank)
-        def _(other=other):
-            greet(device(x, z, core, other))
-
-    takes_far = jnp.logical_and(jnp.logical_and(first, r < NEAR // 2), has_rows)
-
-    @pl.when(takes_far)
-    def _():
-        for group in range(1, GROUPS):
-            for p in range(PIECES):
-                greet(owner_in(group, jnp.int32(p)))
-
     @pl.when(is_owner)
     def _():
         for j in range(MEMBERS):
             @pl.when(jnp.logical_or(j // 2 < owner_base, j // 2 > owner_base + 1))
             def _(j=j):
                 greet(member_device(j))
+
+    for k in range(1, NY):
+        other = lax.rem(y + k, NY)
+        rank = jnp.where(other < NY // 2, other, NY + NY // 2 - 1 - other)
+
+        @pl.when(rank > y_rank)
+        def _(other=other):
+            greet(device(x, z, core, other))
+
+    takes_far = jnp.logical_and(jnp.logical_and(first, r < NEAR // 2), has_rows)
+
+    @pl.when(takes_far)
+    def _():
+        for group in range(1, GROUPS):
+            for p in range(PIECES):
+                greet(owner_in(group, jnp.int32(p)))
+
+    @pl.when(is_owner)
+    def _():
         for k in range(1, NX):
             @pl.when(x + k < NX)
             def _(k=k):
@@ -143,7 +147,7 @@
 
     expected = y_rank + jnp.where(
         is_owner,
-        MEMBERS - 1 + x + g + jnp.where(jnp.logical_and(g >= 1, has_rows), NEAR, 0),
+        PIECES - 1 + 2 * owner_base + x + g + jnp.where(jnp.logical_and(g >= 1, has_rows), NEAR, 0),
         PIECES)
 
     loads[2].wait()
@@ -192,6 +196,11 @@
                     ready(x_ready, device(src, z, core, y))
 
     def answer():
+        for p in range(PIECES):
+            @pl.when(is_late)
+            def _(p=p):
+                ready(back_ready, owner_device(jnp.int32(p)))
+
         earlier_y(lambda dev: ready(y_ready, dev))
 
         @pl.when(jnp.logical_and(is_owner, g >= 1))
@@ -224,15 +233,14 @@
             for seg in range(1, SEGS):
                 s = s * leap[m] + states[seg * PM + i]
             ends[m] = s
-        if n_piece == 1:
+        if n_piece == 0:
             pl.semaphore_wait(barrier, expected)
-        if n_piece >= 1:
-            for ready_piece in order[0 if n_piece == 1 else n_piece:n_piece + 1]:
+            answer_rows()
+        if True:
+            for ready_piece in (p,):
                 @pl.when(jnp.logical_not(is_me(ready_piece)))
                 def _(p=ready_piece):
                     fwd_copy(p).start()
-        if n_piece == 1:
-            answer_rows()
     answer()
 
     loads[4].wait()
@@ -404,6 +412,7 @@
                 for i in range(PM):
                     carry[my_piece, i] = back_src[j, i]
 
+        pl.semaphore_wait(back_ready, MEMBERS - PIECES - 2 * owner_base)
         for j in range(MEMBERS):
             for i in range(PM):
                 if j == 0:
@@ -649,7 +658,8 @@
             dma((MEMBERS,)), dma((2, PIECES)),
             dma((MEMBERS,)), dma((PIECES,)),
             dma((NY - 1,)), dma((NY,)),
-            pltpu.SemaphoreType.REGULAR, pltpu.SemaphoreType.REGULAR, pltpu.SemaphoreType.REGULAR,
+            pltpu.SemaphoreType.REGULAR, pltpu.SemaphoreType.REGULAR,
+            pltpu.SemaphoreType.REGULAR, pltpu.SemaphoreType.REGULAR,
         ],
         compiler_params=pltpu.CompilerParams(collective_id=0, has_side_effects=True),
     )(query, keys, values, rates, residues, skip.reshape(LB, LANES), gain.reshape(LB, LANES))

time: 34.7 us -> 34.4 us (level)
  Pallas kernels: 34.6 us -> 34.1 us
    pallas_call x1, Pallas kernels: 33.8 us -> 33.3 us  [body(): pl.pallas_call(kernel, name='modal_scan', out_shape=(vmem((COUNT, WIDTH),...]
where the time goes in v6:
time: 34.4 us; the launch traced here: 34.1 us
  Pallas kernels  34.1 us (99%)
    pallas_call x1, Pallas kernels, body(): pl.pallas_call(kernel, name='modal_scan', out_shape=(vmem((COUNT, WIDTH),...  33.3 us
    pallas_call x1, Pallas kernels, body(): pl.pallas_call(scale_rows, name='scale_rows', out_shape=jax.ShapeDtypeStr...  0.81 us

profile of v6, /device:TPU:6, one launch (start us, length us, event | category | flops | bytes accessed | tf_op | source)
XLA Modules:
  0.0 34.1 jit_solution(8690772919910190938)
XLA Ops:
  0.0 33.3 %modal_scan.1 = (f32[128,1024]{1,0:T(8,128)S(1)}, f32[8,128]{1,0:T(8,128)S(1)}) custom-call(bf16[128,1024]{1,0:T(8,128)(2,1)} %q_hbm.1, bf16[128,1024]{1,0:T(8,128)(2,1)} %k_hbm.1, bf16[128,1024]{1,0:T(8,128)(2,1)} %v_hbm.1, f32[16,1024]{1,0:T(8,128)} %rates_hbm.1, f32[16,1024]{1,0:T(8,128)} %res_hbm.1, f32[8,128]{1,0:T(8,128)} %bitcast.2, f32[8,128]{1,0:T(8,128)} %bitcast.3), custom_call_target="tpu_custom_call" | custom-call | tf_op jit(solution)/shard_map/modal_scan/pallas_call | solution.py:616
  33.3 0.8 %scale_rows.1 = bf16[128,1024]{1,0:T(8,128)(2,1)} custom-call(f32[128,1024]{1,0:T(8,128)S(1)} %get-tuple-element.7.g_ref, f32[8,128]{1,0:T(8,128)S(1)} %get-tuple-element.8.inv_ref), custom_call_target="tpu_custom_call" | custom-call | tf_op jit(solution)/shard_map/scale_rows/pallas_call | solution.py:666

commit v7 on v6

--- a/solution.py
+++ b/solution.py
@@ -26,6 +26,7 @@
 NEAR = 4
 SCALE_STEPS = 4
 SEG_BLOCKS = BLOCKS // SEGS
+SEG_LOG = (COUNT // SEGS).bit_length() - 1
 
 
 def token_row(block, s):
@@ -34,7 +35,7 @@
 
 def kernel(q_hbm, k_hbm, v_hbm, rates_hbm, res_hbm, skip_hbm, gain_hbm, g_ref, inv_ref,
            q_ref, k_ref, v_ref, rates_ref, res_ref, skip_ref, gain_ref,
-           driven, relay, dec, scale, leap, ends, fwd_buf, total, x_buf, rows_before, rows_with,
+           driven, relay, dec, scale, ends, fwd_buf, total, x_buf, rows_before, rows_with,
            ex_buf, far_buf, far_coef, coef,
            start_state, back_src, carry, query, conv, base, squares, part, parts,
            in_sem, fwd_send, fwd_recv, x_send, x_recv, ex_send, ex_recv, far_send, far_recv,
@@ -79,7 +80,7 @@
 
     loads = []
     for n, (src, dst) in enumerate((
-            (k_hbm, k_ref), (v_hbm, v_ref), (rates_hbm, rates_ref), (res_hbm, res_ref),
+            (rates_hbm, rates_ref), (k_hbm, k_ref), (v_hbm, v_ref), (res_hbm, res_ref),
             (q_hbm, q_ref), (skip_hbm, skip_ref), (gain_hbm, gain_ref))):
         load = pltpu.make_async_copy(src, dst, in_sem.at[n])
         load.start()
@@ -150,25 +151,22 @@
         PIECES - 1 + 2 * owner_base + x + g + jnp.where(jnp.logical_and(g >= 1, has_rows), NEAR, 0),
         PIECES)
 
-    loads[2].wait()
-    loads[3].wait()
-    for which, (src, dst) in enumerate(((rates_ref, dec), (res_ref, scale))):
+    def by_mode(src, top):
         for b in range(M // 8):
             for j in range(LB):
-                relay[which * 128 + (b * 8 + j) * 8:which * 128 + (b * 8 + j) * 8 + 8, :] = (
-                    src[b * 8:b * 8 + 8, j * LANES:(j + 1) * LANES])
+                at = top + (b * 8 + j) * 8
+                relay[at:at + 8, :] = src[b * 8:b * 8 + 8, j * LANES:(j + 1) * LANES]
 
     def mode_rate(m):
         return relay[token_row(m // 8, m % 8), :]
 
+    loads[0].wait()
+    by_mode(rates_ref, 0)
     for m in range(M):
-        d = jnp.exp(-mode_rate(m))
-        dec[m] = d
-        leap[m] = jnp.exp(-mode_rate(m) * (COUNT // SEGS))
-        scale[m] = relay[pl.ds(128 + (m // 8) * 64 + m % 8, 8, stride=8), :] * jnp.sqrt(1.0 - d * d)
-
-    loads[0].wait()
+        dec[m] = jnp.exp(-mode_rate(m))
+
     loads[1].wait()
+    loads[2].wait()
 
     def make_driven(b, _):
         rows = pl.ds(pl.multiple_of(b * 16, 16), 16)
@@ -228,11 +226,13 @@
         zero = jnp.zeros((8, LANES), F32)
         states = lax.fori_loop(0, SEG_BLOCKS, steps, (zero,) * (SEGS * PM))
         for i in range(PM):
-            m = p * PM + i
+            leap = decays[i]
+            for _ in range(SEG_LOG):
+                leap = leap * leap
             s = states[i]
             for seg in range(1, SEGS):
-                s = s * leap[m] + states[seg * PM + i]
-            ends[m] = s
+                s = s * leap + states[seg * PM + i]
+            ends[p * PM + i] = s
         if n_piece == 0:
             pl.semaphore_wait(barrier, expected)
             answer_rows()
@@ -242,6 +242,12 @@
                 def _(p=ready_piece):
                     fwd_copy(p).start()
     answer()
+
+    loads[3].wait()
+    by_mode(res_ref, 128)
+    for m in range(M):
+        d = dec[m]
+        scale[m] = relay[pl.ds(128 + (m // 8) * 64 + m % 8, 8, stride=8), :] * jnp.sqrt(1.0 - d * d)
 
     loads[4].wait()
     loads[5].wait()
@@ -629,7 +635,6 @@
             vmem(tile, F32),
             vmem((COUNT * 8, LANES), F32),
             vmem((256, LANES), F32),
-            vmem((M,) + tile, F32),
             vmem((M,) + tile, F32),
             vmem((M,) + tile, F32),
             vmem((M,) + tile, F32),

time: 34.4 us -> 34.4 us (level)
  no operation moved by 1% of the time
where the time goes in v7:
time: 34.4 us; the launch traced here: 34.1 us
  Pallas kernels  34.1 us (99%)
    pallas_call x1, Pallas kernels, body(): pl.pallas_call(kernel, name='modal_scan', out_shape=(vmem((COUNT, WIDTH),...  33.3 us
    pallas_call x1, Pallas kernels, body(): pl.pallas_call(scale_rows, name='scale_rows', out_shape=jax.ShapeDtypeStr...  0.81 us

profile of v7, /device:TPU:6, one launch (start us, length us, event | category | flops | bytes accessed | tf_op | source)
XLA Modules:
  0.0 34.1 jit_solution(16975211011262377164)
XLA Ops:
  0.0 33.3 %modal_scan.1 = (f32[128,1024]{1,0:T(8,128)S(1)}, f32[8,128]{1,0:T(8,128)S(1)}) custom-call(bf16[128,1024]{1,0:T(8,128)(2,1)} %q_hbm.1, bf16[128,1024]{1,0:T(8,128)(2,1)} %k_hbm.1, bf16[128,1024]{1,0:T(8,128)(2,1)} %v_hbm.1, f32[16,1024]{1,0:T(8,128)} %rates_hbm.1, f32[16,1024]{1,0:T(8,128)} %res_hbm.1, f32[8,128]{1,0:T(8,128)} %bitcast.2, f32[8,128]{1,0:T(8,128)} %bitcast.3), custom_call_target="tpu_custom_call" | custom-call | tf_op jit(solution)/shard_map/modal_scan/pallas_call | solution.py:622
  33.3 0.8 %scale_rows.1 = bf16[128,1024]{1,0:T(8,128)(2,1)} custom-call(f32[128,1024]{1,0:T(8,128)S(1)} %get-tuple-element.7.g_ref, f32[8,128]{1,0:T(8,128)S(1)} %get-tuple-element.8.inv_ref), custom_call_target="tpu_custom_call" | custom-call | tf_op jit(solution)/shard_map/scale_rows/pallas_call | solution.py:671
